TPU v7x, 128 devices: a whole 4x4x4 slice. The times are simulated.
128 devices in a mesh: group: 8 (over y_hi, z), tile: 16 (over x, y_lo, core).
Axes of the slice: x: 4, y: 4 (y_hi: 2, y_lo: 2; y = y_hi * 2 + y_lo), z: 4, core: 2. Of those that a mesh axis runs over, the one named last changes fastest.
Arguments:
- contrast: bfloat16 [8192, 1024], P('tile', 'group'), may hold values from -6 to 6
- incident: bfloat16 [8, 8, 8192, 1024], P('group', None, 'tile'), may hold values from -2.5 to 2.5
- signs: int32 [8, 8, 8], P('group'), may hold values from -1 to 1, as said below
- adjoint: bfloat16 [8, 8, 8192, 1024], P('group', None, 'tile'), may hold values from -1 to 1
- proj: bfloat16 [1024, 256], replicated, may hold values from -0.1875 to 0.1875
- mats: bfloat16 [6, 256, 256], replicated, may hold values from -0.15625 to 0.15625
- offsets: int32 [6], replicated, may hold values from -3 to 3, as said below
- expand: bfloat16 [256, 1024], replicated, may hold values from -0.375 to 0.375
Outputs:
- scattered: bfloat16 [8, 8, 8192, 1024], P('group', None, 'tile')
- gradient: float32 [8192, 1024], P('tile', 'group')
Inputs may be any that keep to these rules, and one draw needn't show every extreme that they name: `signs`: each entry is -1 or 1. The offsets are distinct; -3 and 3 both occur.
All inputs are finite; a program needn't handle non-finite values.
Results may differ from a plain program's by a relative error of at most 0.015.
Values may be sent and summed in bfloat16 or wider, within the bound.
A program may use at most 192 MiB of HBM per device.

v0:
```python
import jax
import jax.numpy as jnp
from jax import lax
from jax.sharding import PartitionSpec as P


def with_halo(block, sides, width):
    for axis, dim in sides:
        count = lax.axis_size(axis)
        forward = [(i, i + 1) for i in range(count - 1)]
        backward = [(target, source) for source, target in forward]
        low = lax.ppermute(
            lax.slice_in_dim(block, block.shape[dim] - width, None, axis=dim), axis, forward
        )
        high = lax.ppermute(lax.slice_in_dim(block, 0, width, axis=dim), axis, backward)
        block = jnp.concatenate([low, block, high], axis=dim)
    return block


def translate(padded, mats, offsets):
    count = mats.shape[0]
    rows = padded.shape[0]
    nbox = padded.shape[1] - 6
    width = mats.shape[2]
    total = jnp.zeros((rows, nbox, width), jnp.float32)
    for t in range(count):
        moved = lax.dynamic_slice_in_dim(padded, offsets[t] + 3, nbox, 1)
        total = total + jnp.dot(
            moved.reshape(-1, width), mats[t], preferred_element_type=jnp.float32
        ).reshape(rows, nbox, width)
    return total


def on_device(contrast, incident, signs, adjoint, proj, mats, offsets, expand):
    full_contrast = lax.all_gather(contrast, "group", axis=1, tiled=True)
    nbox = full_contrast.shape[0]
    points = full_contrast.shape[1]
    width = proj.shape[1]
    encoded = jnp.einsum(
        "es,sbp->ebp",
        signs[0].astype(jnp.bfloat16),
        incident[0],
        preferred_element_type=jnp.float32,
    ).astype(jnp.bfloat16)
    rows = encoded.shape[0]
    adjoint_f = adjoint[0].astype(jnp.float32)
    source = (full_contrast.astype(jnp.float32)[None] * encoded.astype(jnp.float32)).astype(
        jnp.bfloat16
    )
    coeffs = (
        jnp.dot(source.reshape(-1, points), proj, preferred_element_type=jnp.float32)
        .reshape(rows, nbox, width)
        .astype(jnp.bfloat16)
    )
    padded = with_halo(coeffs, (("tile", 1),), 3)
    local = translate(padded, mats, offsets).astype(jnp.bfloat16)
    field = jnp.dot(local.reshape(-1, width), expand, preferred_element_type=jnp.float32).reshape(
        rows, nbox, points
    )
    total = encoded.astype(jnp.float32) + field
    terms = jnp.sum(adjoint_f * total, axis=0)
    gradient = lax.psum_scatter(terms, "group", scatter_dimension=1, tiled=True)
    return (field.astype(jnp.bfloat16)[None], gradient)


def solution(mesh):
    in_specs = (
        P("tile", "group"),
        P("group", None, "tile", None),
        P("group", None, None),
        P("group", None, "tile", None),
        P(),
        P(),
        P(),
        P(),
    )
    out_specs = (P("group", None, "tile", None), P("tile", "group"))
    return jax.shard_map(
        on_device, mesh=mesh, in_specs=in_specs, out_specs=out_specs, check_vma=False
    )
```

profile of v0, /device:TPU:0, one launch (start us, length us, event | category | flops | bytes accessed | tf_op | source)
XLA Modules:
  0.0 242.7 jit_solution(2367427757209642867)
XLA Ops:
  7.2 0.0 copy-start
  7.2 0.0 all-gather.2.cloned.1.call-start
  7.2 0.7 all-gather.2.cloned.1.call-update
  7.9 0.0 reduce-scatter.2.cloned.1.call-start
  8.0 50.0 %all-gather.2.cloned.1.call-done = bf16[512,1024]{1,0:T(8,128)(2,1)} async-done(((bf16[512,128]{1,0:T(8,128)(2,1)}), bf16[512,1024]{1,0:T(8,128)(2,1)}) %all-gather.2.cloned.1.call-update) | async-done | bytes 1048592 | tf_op jit(solution)/shard_map/all_gather | solution.py:35
  58.0 1.5 convert_element_type.34
  59.5 0.0 copy-start.5
  59.5 12.4 %fusion = (bf16[8,512,1024]{2,0,1:T(8,128)(2,1)}, bf16[8,512,1024]{2,0,1:T(8,128)(2,1)}) fusion(f32[512,1024]{1,0:T(8,128)S(1)} %convert_element_type.34, bf16[8,512,1024]{2,1,0:T(8,128)(2,1)} %bitcast.55, s32[1,8,8]{2,1,0:T(8,128)} %param.10), kind=kOutput, calls=%fused_computation.2 | convolution fusion | flops 83886144 | bytes 27263232 | tf_op jit(solution)/shard_map/es,sbp->ebp/dot_general | solution.py:39
  71.9 0.0 copy-done.5
  71.9 0.0 copy-start.4
  71.9 12.9 %fusion.25 = bf16[8,512,256]{2,1,0:T(8,128)(2,1)S(1)} fusion(bf16[8,512,1024]{2,0,1:T(8,128)(2,1)} %get-tuple-element.10, bf16[1024,256]{1,0:T(8,128)(2,1)S(1)} %copy-done.5), kind=kOutput, calls=%fused_computation.26 | convolution fusion | flops 2148532224 | bytes 11010048 | tf_op jit(solution)/shard_map/dot_general | solution.py:51
  84.8 0.0 copy-start.2
  84.8 1.3 copy-done.2
  86.1 0.0 copy-start.3
  86.1 1.4 collective-permute-start
  87.5 1.5 collective-permute-start.1
  89.1 0.0 copy-done.4
  89.1 0.7 fusion.54
  97.3 0.0 collective-permute-done
  97.3 0.0 collective-permute-done.1
  97.3 2.1 pad_maximum_fusion
  99.4 0.0 copy-done.3
  99.4 2.7 %fusion.15 = f32[8,512,256]{2,1,0:T(8,128)} fusion(bf16[8,518,256]{2,1,0:T(8,128)(2,1)S(1)} %pad_maximum_fusion, s32[]{:T(128)S(6)} %select_n.22, bf16[6,256,256]{2,1,0:T(8,128)(2,1)S(1)} %copy-done.3), kind=kOutput, calls=%fused_computation.16 | convolution fusion | flops 536870912 | bytes 6422532 | tf_op jit(solution)/shard_map/dot_general | solution.py:28
  102.2 2.7 %fusion.17 = f32[8,512,256]{2,1,0:T(8,128)} fusion(bf16[8,518,256]{2,1,0:T(8,128)(2,1)S(1)} %pad_maximum_fusion, s32[]{:T(128)S(6)} %select_n.21, bf16[6,256,256]{2,1,0:T(8,128)(2,1)S(1)} %copy-done.3), kind=kOutput, calls=%fused_computation.18 | convolution fusion | flops 536870912 | bytes 6422532 | tf_op jit(solution)/shard_map/dot_general | solution.py:28
  104.9 2.6 %fusion.19 = f32[8,512,256]{2,1,0:T(8,128)} fusion(bf16[8,518,256]{2,1,0:T(8,128)(2,1)S(1)} %pad_maximum_fusion, s32[]{:T(128)S(6)} %select_n.20, bf16[6,256,256]{2,1,0:T(8,128)(2,1)S(1)} %copy-done.3), kind=kOutput, calls=%fused_computation.20 | convolution fusion | flops 536870912 | bytes 6422532 | tf_op jit(solution)/shard_map/dot_general | solution.py:28
  107.5 2.7 %fusion.21 = f32[8,512,256]{2,1,0:T(8,128)} fusion(bf16[8,518,256]{2,1,0:T(8,128)(2,1)S(1)} %pad_maximum_fusion, s32[]{:T(128)S(6)} %select_n.19, bf16[6,256,256]{2,1,0:T(8,128)(2,1)S(1)} %copy-done.3), kind=kOutput, calls=%fused_computation.22 | convolution fusion | flops 536870912 | bytes 6422532 | tf_op jit(solution)/shard_map/dot_general | solution.py:28
  110.2 2.8 %fusion.23 = f32[8,512,256]{2,1,0:T(8,128)} fusion(bf16[8,518,256]{2,1,0:T(8,128)(2,1)S(1)} %pad_maximum_fusion, s32[]{:T(128)S(6)} %select_n.18, bf16[6,256,256]{2,1,0:T(8,128)(2,1)S(1)} %copy-done.3), kind=kOutput, calls=%fused_computation.24 | convolution fusion | flops 536870912 | bytes 6422532 | tf_op jit(solution)/shard_map/dot_general | solution.py:28
  113.0 0.0 copy-done
  113.0 12.4 %fusion.10 = f32[8,512,1024]{2,1,0:T(8,128)} fusion(f32[8,512,256]{2,1,0:T(8,128)} %fusion.15, f32[8,512,256]{2,1,0:T(8,128)} %fusion.17, f32[8,512,256]{2,1,0:T(8,128)} %fusion.19, f32[8,512,256]{2,1,0:T(8,128)} %fusion.23, f32[8,512,256]{2,1,0:T(8,128)} %fusion.21, bf16[8,518,256]{2,1,0:T(8,128)(2,1)S(1)} %pad_maximum_fusion, s32[]{:T(128)S(6)} %select_n.23, ...), kind=kOutput, calls=%fused_computation.13 | convolution fusion | flops 2690646016 | bytes 40501252 | tf_op jit(solution)/shard_map/dot_general | solution.py:57
  125.4 32.0 %fusion.2 = f32[512,1024]{1,0:T(8,128)} fusion(bf16[8,512,1024]{2,0,1:T(8,128)(2,1)} %get-tuple-element.11, f32[8,512,1024]{2,1,0:T(8,128)} %fusion.10, bf16[1,8,512,1024]{3,2,1,0:T(8,128)(2,1)} %param.11), kind=kLoop, calls=%fused_computation.4 | loop fusion | flops 20447232 | bytes 35651584 | tf_op jit(solution)/shard_map/reduce_sum | solution.py:61
  157.4 0.0 reduce-scatter.2.cloned.1.call-update
  157.4 0.0 copy-start.1
  157.4 9.1 %convert_bitcast_fusion = bf16[1,8,512,1024]{3,2,1,0:T(8,128)(2,1)} fusion(f32[8,512,1024]{2,1,0:T(8,128)} %fusion.10), kind=kLoop, calls=%fused_computation.9 | loop fusion | flops 4194304 | bytes 25165824 | tf_op jit(solution)/shard_map/broadcast_in_dim | solution.py:63
  166.5 69.3 %reduce-scatter.2.cloned.1.call-done = f32[512,128]{1,0:T(8,128)} async-done(((f32[512,1024]{1,0:T(8,128)}), f32[512,128]{1,0:T(8,128)}) %reduce-scatter.2.cloned.1.call-update) | async-done | bytes 262160 | tf_op jit(solution)/shard_map/reduce_scatter | solution.py:62
  235.8 0.0 copy-done.1
  (1 shorter events, 0.0 us)
Async XLA Ops:
  7.2 105.8 %copy-start = (bf16[256,1024]{1,0:T(8,128)(2,1)S(1)}, bf16[256,1024]{1,0:T(8,128)(2,1)}, u32[]{:S(2)}) copy-start(bf16[256,1024]{1,0:T(8,128)(2,1)} %param.15) | copy-start | bytes 1572868
  7.2 50.8 %all-gather.2.cloned.1.call-start = ((), (), s32[]{:S(2)}) async-start(), calls=%async_computation.1 | async-start | bytes 1179648 | tf_op jit(solution)/shard_map/all_gather | solution.py:35
  7.9 227.9 %reduce-scatter.2.cloned.1.call-start = ((), (), s32[]{:S(2)}) async-start(), calls=%async_computation.2 | async-start | bytes 2359296 | tf_op jit(solution)/shard_map/reduce_scatter | solution.py:62
  59.5 12.4 %copy-start.5 = (bf16[1024,256]{1,0:T(8,128)(2,1)S(1)}, bf16[1024,256]{1,0:T(8,128)(2,1)}, u32[]{:S(2)}) copy-start(bf16[1024,256]{1,0:T(8,128)(2,1)} %param.12) | copy-start | bytes 1572868
  71.9 17.2 %copy-start.4 = (s32[6]{0:T(128)S(1)}, s32[6]{0:T(128)}, u32[]{:S(2)}) copy-start(s32[6]{0:T(128)} %param.14) | copy-start | bytes 76
  84.8 1.3 copy-start.2
  86.1 13.3 %copy-start.3 = (bf16[6,256,256]{2,1,0:T(8,128)(2,1)S(1)}, bf16[6,256,256]{2,1,0:T(8,128)(2,1)}, u32[]{:S(2)}) copy-start(bf16[6,256,256]{2,1,0:T(8,128)(2,1)} %param.13) | copy-start | bytes 2359300
  86.1 11.2 %collective-permute-start = (bf16[8,3,256]{2,1,0:T(4,128)(2,1)S(1)}, bf16[8,3,256]{2,1,0:T(4,128)(2,1)S(1)}, u32[]{:S(2)}, u32[]{:S(2)}) collective-permute-start(bf16[8,3,256]{2,1,0:T(4,128)(2,1)S(1)} %get-tuple-element.2), channel_id=1, source_target_pairs={{0,1},{1,2},{2,3},{3,4},{4,5},{5,6},{6,7},{7,8},{8,9},{9,10},{10,1... | collective-permute-start | bytes 36872 | tf_op jit(solution)/shard_map/ppermute | solution.py:12
  87.5 9.8 %collective-permute-start.1 = (bf16[8,3,256]{2,1,0:T(4,128)(2,1)S(1)}, bf16[8,3,256]{2,1,0:T(4,128)(2,1)S(1)}, u32[]{:S(2)}, u32[]{:S(2)}) collective-permute-start(bf16[8,3,256]{2,1,0:T(4,128)(2,1)S(1)} %get-tuple-element.3), channel_id=1, source_target_pairs={{1,0},{2,1},{3,2},{4,3},{5,4},{6,5},{7,6},{8,7},{9,8},{10,9},{11,1... | collective-permute-start | bytes 36872 | tf_op jit(solution)/shard_map/ppermute | solution.py:15
  157.4 78.4 %copy-start.1 = (bf16[256,1024]{1,0:T(8,128)(2,1)S(1)}, bf16[256,1024]{1,0:T(8,128)(2,1)}, u32[]{:S(2)}) copy-start(bf16[256,1024]{1,0:T(8,128)(2,1)} %param.15) | copy-start | bytes 1572868
Sparse Core Ops, SparseCore 0:
  10.2 47.7 all-gather.1
  157.5 78.2 reduce-scatter.1
where the time goes:
time: 243 us
  waiting for transfers between devices  120 us (49%)
  matrix products  51.2 us (21%)
  other arithmetic  44.6 us (18%)
  between operations  21.7 us (9%)
  starting transfers between devices  3.01 us (1%)
    reduce_scatter x1, waiting for transfers between devices, on_device(): gradient = lax.psum_scatter(terms, 'group', scatter_dimension=1, tiled=True)  69.3 us
    all_gather x1, waiting for transfers between devices, on_device(): full_contrast = lax.all_gather(contrast, 'group', axis=1, tiled=True)  50 us
    reduce_sum x1, other arithmetic, on_device(): terms = jnp.sum(adjoint_f * total, axis=0)  32 us
    dot_general x5, matrix products, translate(): jnp.dot(moved.reshape(-1, width), mats[t], preferred_element_type=jnp.flo...  13.5 us
    dot_general x1, matrix products, on_device(): jnp.dot(source.reshape(-1, points), proj, preferred_element_type=jnp.floa...  12.9 us
    dot_general x1, matrix products, on_device(): jnp.einsum('es,sbp->ebp', signs[0].astype(jnp.bfloat16), incident[0], pre...  12.4 us
    dot_general x1, matrix products, on_device(): jnp.dot(local.reshape(-1, width), expand, preferred_element_type=jnp.floa...  12.4 us
    broadcast_in_dim x1, other arithmetic, on_device(): return (field.astype(jnp.bfloat16)[None], gradient)  9.13 us
  transfers between devices with their start and end apart: 4, of which 2 were waited for; matrix products, arithmetic and copies ran while one was open for 4% of the time, Pallas kernels for 0%

commit v1 on v0

v1 whole, which is shorter than its diff:
```python
import jax
import jax.numpy as jnp
from jax import lax
from jax.experimental import pallas as pl
from jax.experimental.pallas import tpu as pltpu
from jax.sharding import PartitionSpec as P

MESH = pl.DeviceIdType.MESH
BF = jnp.bfloat16
F32 = jnp.float32

S = 8
K = 256
PTS = 1024
NB = 512
HB = 32
TB = 64
NT = NB // TB
NG = 8
GW = PTS // NG
PAD = 8
CW = 256
NC = PTS // CW
REACH = 3
ND = 2 * REACH + 1


def scatter_gradient_kernel(
    signs, offsets, con_hbm, inc_hbm, adj_hbm, proj, mats, expand,
    loc_hbm, part_hbm,
    con_v, inc_v, enc_v, adj_v, coef_v, loc_v, term_v, kron, shifts,
    in_sem, con_sem, adj_sem, loc_sem, own_sem,
    ag_send, ag_recv, rs_send, rs_recv, halo_send, halo_recv,
):
    g = lax.axis_index("group")
    tile = lax.axis_index("tile")
    last = lax.axis_size("tile") - 1

    def rows_of(t):
        return pl.ds(pl.multiple_of(t * TB, TB), TB)

    def inc_copy(t):
        r = rows_of(t)
        return pltpu.make_async_copy(inc_hbm.at[:, r], inc_v.at[:, r], in_sem.at[t])

    def adj_copy(t):
        r = rows_of(t)
        return pltpu.make_async_copy(adj_hbm.at[:, r], adj_v.at[:, r], adj_sem.at[t])

    mine = pl.ds(pl.multiple_of(g * GW, GW), GW)
    con_copy = pltpu.make_async_copy(con_hbm, con_v.at[:, mine], con_sem)

    def ag_copy(t, k):
        return pltpu.make_async_remote_copy(
            src_ref=con_hbm.at[rows_of(t)],
            dst_ref=con_v.at[rows_of(t), mine],
            send_sem=ag_send.at[t, k - 1],
            recv_sem=ag_recv.at[t, k - 1],
            device_id=(lax.rem(g + k, NG), tile),
            device_id_type=MESH,
        )

    def rs_copy(t, k):
        peer = lax.rem(g + k, NG)
        return pltpu.make_async_remote_copy(
            src_ref=term_v.at[peer, rows_of(t)],
            dst_ref=part_hbm.at[g, rows_of(t)],
            send_sem=rs_send.at[t, k - 1],
            recv_sem=rs_recv.at[t, k - 1],
            device_id=(peer, tile),
            device_id_type=MESH,
        )

    def own_copy(t):
        r = rows_of(t)
        return pltpu.make_async_copy(term_v.at[g, r], part_hbm.at[g, r], own_sem.at[t])

    def loc_copy(t):
        r = rows_of(t)
        return pltpu.make_async_copy(loc_v.at[:, r], loc_hbm.at[:, r], loc_sem.at[t])

    def halo_up():
        return pltpu.make_async_remote_copy(
            src_ref=coef_v.at[:, pl.ds(NB, PAD)],
            dst_ref=coef_v.at[:, pl.ds(0, PAD)],
            send_sem=halo_send.at[0],
            recv_sem=halo_recv.at[0],
            device_id=(g, tile + 1),
            device_id_type=MESH,
        )

    def halo_down():
        return pltpu.make_async_remote_copy(
            src_ref=coef_v.at[:, pl.ds(PAD, PAD)],
            dst_ref=coef_v.at[:, pl.ds(NB + PAD, PAD)],
            send_sem=halo_send.at[1],
            recv_sem=halo_recv.at[1],
            device_id=(g, tile - 1),
            device_id_type=MESH,
        )

    def tile_at(j):
        return jnp.where(j == 0, 0, jnp.where(j == 1, NT - 1, j - 1))

    con_copy.start()
    inc_copy(0).start()
    inc_copy(NT - 1).start()
    for t in range(1, NT - 1):
        inc_copy(t).start()
    for t in list(range(1, NT - 1)) + [0, NT - 1]:
        adj_copy(t).start()

    barrier = pltpu.get_barrier_semaphore()
    for k in range(1, NG):
        pl.semaphore_signal(
            barrier, inc=1, device_id=(lax.rem(g + k, NG), tile), device_id_type=MESH
        )

    for step_of in (1, last):
        pl.semaphore_signal(
            barrier, inc=1, device_id=(g, lax.rem(tile + step_of, last + 1)), device_id_type=MESH
        )
    pl.semaphore_wait(barrier, NG + 1)

    def ag_start(j, carry):
        for k in range(1, NG):
            ag_copy(tile_at(j), k).start()
        return carry

    lax.fori_loop(0, NT, ag_start, 0)

    lane = lax.broadcasted_iota(jnp.int32, (HB, S * HB), 1)
    row = lax.broadcasted_iota(jnp.int32, (HB, S * HB), 0)
    diag = lax.rem(lane, HB) == row
    source = lane // HB
    for e in range(S):
        value = jnp.zeros((HB, S * HB), F32)
        for s in range(S):
            value = jnp.where(source == s, signs[e, s].astype(F32), value)
        kron[pl.ds(e * HB, HB), :] = jnp.where(diag, value, 0.0).astype(BF)

    for d in range(ND):
        found = jnp.int32(0)
        where = jnp.int32(0)
        for t in range(mats.shape[0]):
            hit = offsets[t] == d - REACH
            found = jnp.where(hit, 1, found)
            where = jnp.where(hit, t, where)
        shifts[d] = (mats[where].astype(F32) * found.astype(F32)).astype(BF)

    @pl.when(tile == 0)
    def _():
        coef_v[:, 0:PAD, :] = jnp.zeros((S, PAD, K), F32)

    @pl.when(tile == last)
    def _():
        coef_v[:, NB + PAD : NB + 2 * PAD, :] = jnp.zeros((S, PAD, K), F32)

    con_copy.wait()

    def project(t):
        inc_copy(t).wait()
        for k in range(1, NG):
            ag_copy(t, k).wait_recv()
        for h in range(TB // HB):
            b0 = pl.multiple_of(t * TB + h * HB, HB)
            boxes = pl.ds(b0, HB)
            acc = jnp.zeros((S * HB, K), F32)
            for c in range(NC):
                cols = pl.ds(c * CW, CW)
                enc = jnp.dot(
                    kron[...],
                    inc_v[:, boxes, cols].reshape(S * HB, CW),
                    preferred_element_type=F32,
                ).astype(BF).reshape(S, HB, CW)
                enc_v[:, boxes, cols] = enc
                src = enc * con_v[boxes, cols][None]
                acc = acc + jnp.dot(
                    src.reshape(S * HB, CW), proj[cols, :], preferred_element_type=F32
                )
            coef_v[:, pl.ds(pl.multiple_of(b0 + PAD, PAD), HB), :] = acc.reshape(S, HB, K)

    def expand_terms(t):
        adj_copy(t).wait()
        for h in range(TB // HB):
            b0 = pl.multiple_of(t * TB + h * HB, HB)
            boxes = pl.ds(b0, HB)
            acc = jnp.zeros((S * HB, K), F32)
            window = coef_v.at[:, pl.ds(b0, HB + 2 * PAD), :]
            for d in range(ND):
                first = PAD + d - REACH
                moved = window[:, first : first + HB, :]
                acc = acc + jnp.dot(
                    moved.astype(BF).reshape(S * HB, K), shifts[d], preferred_element_type=F32
                )
            local = acc.astype(BF)
            loc_v[:, boxes, :] = local.reshape(S, HB, K)
            for c in range(NC):
                cols = pl.ds(c * CW, CW)
                field = jnp.dot(local, expand[:, cols], preferred_element_type=F32)
                total = enc_v[:, boxes, cols].astype(F32) + field.reshape(S, HB, CW)
                term = jnp.sum(adj_v[:, boxes, cols].astype(F32) * total, axis=0).astype(BF)
                for q in range(CW // GW):
                    term_v[c * (CW // GW) + q, boxes, :] = term[:, q * GW : (q + 1) * GW]
        loc_copy(t).start()
        own_copy(t).start()
        for k in range(1, NG):
            rs_copy(t, k).start()

    def step(j, carry):
        @pl.when(j < NT)
        def _():
            project(tile_at(j))

        @pl.when(j == 2)
        def _():
            @pl.when(tile < last)
            def _():
                halo_up().start()

            @pl.when(tile > 0)
            def _():
                halo_down().start()

        @pl.when(j == NT + 1)
        def _():
            @pl.when(tile > 0)
            def _():
                halo_up().wait_recv()

            @pl.when(tile < last)
            def _():
                halo_down().wait_recv()

        @pl.when(j >= 3)
        def _():
            expand_terms(jnp.where(j == NT + 1, 0, jnp.where(j == NT + 2, NT - 1, j - 2)))

        return carry

    lax.fori_loop(0, NT + 3, step, 0)

    def finish(t, carry):
        loc_copy(t).wait()
        own_copy(t).wait()
        for k in range(1, NG):
            ag_copy(t, k).wait_send()
            rs_copy(t, k).wait_send()
            rs_copy(t, k).wait_recv()
        return carry

    lax.fori_loop(0, NT, finish, 0)

    @pl.when(tile < last)
    def _():
        halo_up().wait_send()

    @pl.when(tile > 0)
    def _():
        halo_down().wait_send()


def output_kernel(loc, expand, part, scat, grad):
    n = loc.shape[1]
    for c in range(NC):
        cols = pl.ds(c * CW, CW)
        scat[:, :, cols] = (
            jnp.dot(loc[...].reshape(S * n, K), expand[:, cols], preferred_element_type=F32)
            .astype(BF)
            .reshape(S, n, CW)
        )
    grad[...] = jnp.sum(part[...].astype(F32), axis=0)


def on_device(contrast, incident, signs, adjoint, proj, mats, offsets, expand):
    any_spec = pl.BlockSpec(memory_space=pl.ANY)
    vmem = pl.BlockSpec(memory_space=pltpu.VMEM)
    smem = pl.BlockSpec(memory_space=pltpu.SMEM)
    dma = pltpu.SemaphoreType.DMA
    local, parts = pl.pallas_call(
        scatter_gradient_kernel,
        out_shape=(
            jax.ShapeDtypeStruct((S, NB, K), BF),
            jax.ShapeDtypeStruct((NG, NB, GW), BF),
        ),
        in_specs=[smem, smem, any_spec, any_spec, any_spec, vmem, vmem, vmem],
        out_specs=(any_spec, any_spec),
        scratch_shapes=[
            pltpu.VMEM((NB, PTS), BF),
            pltpu.VMEM((S, NB, PTS), BF),
            pltpu.VMEM((S, NB, PTS), BF),
            pltpu.VMEM((S, NB, PTS), BF),
            pltpu.VMEM((S, NB + 2 * PAD, K), F32),
            pltpu.VMEM((S, NB, K), BF),
            pltpu.VMEM((NG, NB, GW), BF),
            pltpu.VMEM((S * HB, S * HB), BF),
            pltpu.VMEM((ND, K, K), BF),
            dma((NT,)),
            dma,
            dma((NT,)),
            dma((NT,)),
            dma((NT,)),
            dma((NT, NG - 1)),
            dma((NT, NG - 1)),
            dma((NT, NG - 1)),
            dma((NT, NG - 1)),
            dma((2,)),
            dma((2,)),
        ],
        compiler_params=pltpu.CompilerParams(
            collective_id=0, has_side_effects=True, vmem_limit_bytes=60 << 20
        ),
    )(signs[0], offsets, contrast, incident[0], adjoint[0], proj, mats, expand)

    scattered, gradient = pl.pallas_call(
        output_kernel,
        grid=(NT,),
        out_shape=(
            jax.ShapeDtypeStruct((S, NB, PTS), BF),
            jax.ShapeDtypeStruct((NB, GW), F32),
        ),
        in_specs=[
            pl.BlockSpec((S, TB, K), lambda i: (0, i, 0)),
            pl.BlockSpec((K, PTS), lambda i: (0, 0)),
            pl.BlockSpec((NG, TB, GW), lambda i: (0, i, 0)),
        ],
        out_specs=(
            pl.BlockSpec((S, TB, PTS), lambda i: (0, i, 0)),
            pl.BlockSpec((TB, GW), lambda i: (i, 0)),
        ),
        compiler_params=pltpu.CompilerParams(vmem_limit_bytes=60 << 20),
    )(local, expand, parts)
    return scattered[None], gradient


def solution(mesh):
    in_specs = (
        P("tile", "group"),
        P("group", None, "tile", None),
        P("group", None, None),
        P("group", None, "tile", None),
        P(),
        P(),
        P(),
        P(),
    )
    out_specs = (P("group", None, "tile", None), P("tile", "group"))
    return jax.shard_map(
        on_device, mesh=mesh, in_specs=in_specs, out_specs=out_specs, check_vma=False
    )
```

time: 243 us -> 54.7 us (0.23)
  waiting for transfers between devices: 120 us -> 0 us
  Pallas kernels: 0 us -> 53.7 us
  matrix products: 51.2 us -> 0 us
  other arithmetic: 44.6 us -> 0 us
  between operations: 21.7 us -> 0.64 us
  starting transfers between devices: 3.01 us -> 0 us
    reduce_scatter x1 -> x0, waiting for transfers between devices: 69.3 us -> none  [on_device(): gradient = lax.psum_scatter(terms, 'group', scatter_dimension=1, tiled=True)]
    pallas_call x0 -> x2, Pallas kernels: none -> 53.7 us  [the longest x1 44.9 us: on_device(): pl.pallas_call(scatter_gradient_kernel, out_shape=(jax.ShapeDtypeStruct((...]
    dot_general x8 -> x0, matrix products: 51.2 us -> none  [the longest x5 13.5 us: translate(): jnp.dot(moved.reshape(-1, width), mats[t], preferred_element_type=jnp.flo...]
    all_gather x1 -> x0, waiting for transfers between devices: 50 us -> none  [on_device(): full_contrast = lax.all_gather(contrast, 'group', axis=1, tiled=True)]
    reduce_sum x1 -> x0, other arithmetic: 32 us -> none  [on_device(): terms = jnp.sum(adjoint_f * total, axis=0)]
    broadcast_in_dim x1 -> x0, other arithmetic: 9.13 us -> none  [on_device(): return (field.astype(jnp.bfloat16)[None], gradient)]
    ppermute x2 -> x0, starting transfers between devices: 2.93 us -> none  [the longest x1 1.51 us: with_halo(): lax.ppermute(lax.slice_in_dim(block, 0, width, axis=dim), axis, backward)]
  transfers between devices with their start and end apart: 4 -> 0, of which waited for: 2 -> 0; matrix products, arithmetic and copies ran while one was open for 4% -> 0% of each run, Pallas kernels for 0% -> 0%
where the time goes in v1:
time: 54.7 us; the launch traced here: 54.3 us
  Pallas kernels  53.7 us (98%)
  between operations  0.64 us (1%)
    pallas_call x1, Pallas kernels, on_device(): pl.pallas_call(scatter_gradient_kernel, out_shape=(jax.ShapeDtypeStruct((...  44.9 us
    pallas_call x1, Pallas kernels, on_device(): pl.pallas_call(output_kernel, grid=(NT,), out_shape=(jax.ShapeDtypeStruct...  8.8 us

profile of v1, /device:TPU:0, one launch (start us, length us, event | category | flops | bytes accessed | tf_op | source)
XLA Modules:
  0.0 54.3 jit_solution(16418366148349500574)
XLA Ops:
  0.6 44.9 %shard_map.95 = (bf16[8,512,256]{2,1,0:T(8,128)(2,1)}, bf16[8,512,128]{2,1,0:T(8,128)(2,1)}) custom-call(s32[8,8]{1,0:T(8,128)} %bitcast.6, s32[6]{0:T(128)} %offsets.1, bf16[512,128]{1,0:T(8,128)(2,1)} %con_hbm.1, bf16[8,512,1024]{2,1,0:T(8,128)(2,1)} %bitcast.4, bf16[8,512,1024]{2,1,0:T(8,128)(2,1)} %bitcast.5, bf16[1024,256]{1,0:T(8,128)(2,1)} %proj.1, ...), custom_call_target="tpu_custom_call" | custom-call | tf_op jit(solution)/shard_map/pallas_call | solution.py:280
  45.5 8.8 %shard_map.96 = (bf16[8,512,1024]{2,1,0:T(8,128)(2,1)}, f32[512,128]{1,0:T(8,128)}) custom-call(bf16[8,512,256]{2,1,0:T(8,128)(2,1)} %get-tuple-element.6.loc, bf16[256,1024]{1,0:T(8,128)(2,1)} %expand.3, bf16[8,512,128]{2,1,0:T(8,128)(2,1)} %get-tuple-element.7.part), custom_call_target="tpu_custom_call" | custom-call | tf_op jit(solution)/shard_map/pallas_call | solution.py:315

commit v2 on v1

--- a/solution.py
+++ b/solution.py
@@ -14,21 +14,24 @@
 PTS = 1024
 NB = 512
 HB = 32
+ROWS = S * HB
 TB = 64
 NT = NB // TB
 NG = 8
 GW = PTS // NG
-PAD = 8
 CW = 256
 NC = PTS // CW
 REACH = 3
-ND = 2 * REACH + 1
+
+
+def mm(a, b):
+    return jnp.dot(a, b, preferred_element_type=F32)
 
 
 def scatter_gradient_kernel(
     signs, offsets, con_hbm, inc_hbm, adj_hbm, proj, mats, expand,
     loc_hbm, part_hbm,
-    con_v, inc_v, enc_v, adj_v, coef_v, loc_v, term_v, kron, shifts,
+    con_v, inc_v, adj_v, coef_v, low_v, high_v, loc_v, first_v, term_v, enc_points, enc_coeffs, perm,
     in_sem, con_sem, adj_sem, loc_sem, own_sem,
     ag_send, ag_recv, rs_send, rs_recv, halo_send, halo_recv,
 ):
@@ -81,8 +84,8 @@
 
     def halo_up():
         return pltpu.make_async_remote_copy(
-            src_ref=coef_v.at[:, pl.ds(NB, PAD)],
-            dst_ref=coef_v.at[:, pl.ds(0, PAD)],
+            src_ref=coef_v.at[pl.ds(NB, REACH)],
+            dst_ref=low_v,
             send_sem=halo_send.at[0],
             recv_sem=halo_recv.at[0],
             device_id=(g, tile + 1),
@@ -91,8 +94,8 @@
 
     def halo_down():
         return pltpu.make_async_remote_copy(
-            src_ref=coef_v.at[:, pl.ds(PAD, PAD)],
-            dst_ref=coef_v.at[:, pl.ds(NB + PAD, PAD)],
+            src_ref=coef_v.at[pl.ds(REACH, REACH)],
+            dst_ref=high_v,
             send_sem=halo_send.at[1],
             recv_sem=halo_recv.at[1],
             device_id=(g, tile - 1),
@@ -103,11 +106,8 @@
         return jnp.where(j == 0, 0, jnp.where(j == 1, NT - 1, j - 1))
 
     con_copy.start()
-    inc_copy(0).start()
-    inc_copy(NT - 1).start()
-    for t in range(1, NT - 1):
+    for t in [0, NT - 1] + list(range(1, NT - 1)):
         inc_copy(t).start()
-    for t in list(range(1, NT - 1)) + [0, NT - 1]:
         adj_copy(t).start()
 
     barrier = pltpu.get_barrier_semaphore()
@@ -115,11 +115,29 @@
         pl.semaphore_signal(
             barrier, inc=1, device_id=(lax.rem(g + k, NG), tile), device_id_type=MESH
         )
-
     for step_of in (1, last):
         pl.semaphore_signal(
             barrier, inc=1, device_id=(g, lax.rem(tile + step_of, last + 1)), device_id_type=MESH
         )
+
+    lane8 = lax.broadcasted_iota(jnp.int32, (S, ROWS), 1)
+    row8 = lax.broadcasted_iota(jnp.int32, (S, ROWS), 0)
+    sign = jnp.zeros((S, ROWS), F32)
+    for e in range(S):
+        for s in range(S):
+            here = (row8 == e) & (lane8 // HB == s)
+            sign = jnp.where(here, signs[e, s].astype(F32), sign)
+    for b in range(0, HB, 2):
+        pair = [jnp.where(lax.rem(lane8, HB) == b + i, sign, 0.0) for i in range(2)]
+        enc_coeffs[pl.ds(b * S, 2 * S), :] = jnp.concatenate(pair, axis=0).astype(BF)
+    lane = lax.broadcasted_iota(jnp.int32, (HB, ROWS), 1)
+    row = lax.broadcasted_iota(jnp.int32, (HB, ROWS), 0)
+    for e in range(S):
+        wide = jnp.broadcast_to(sign[e : e + 1, :], (HB, ROWS))
+        enc_points[pl.ds(e * HB, HB), :] = jnp.where(lax.rem(lane, HB) == row, wide, 0.0).astype(BF)
+        there = (lane // S == row) & (lax.rem(lane, S) == e)
+        perm[pl.ds(e * HB, HB), :] = jnp.where(there, 1.0, 0.0).astype(BF)
+
     pl.semaphore_wait(barrier, NG + 1)
 
     def ag_start(j, carry):
@@ -129,77 +147,59 @@
 
     lax.fori_loop(0, NT, ag_start, 0)
 
-    lane = lax.broadcasted_iota(jnp.int32, (HB, S * HB), 1)
-    row = lax.broadcasted_iota(jnp.int32, (HB, S * HB), 0)
-    diag = lax.rem(lane, HB) == row
-    source = lane // HB
-    for e in range(S):
-        value = jnp.zeros((HB, S * HB), F32)
-        for s in range(S):
-            value = jnp.where(source == s, signs[e, s].astype(F32), value)
-        kron[pl.ds(e * HB, HB), :] = jnp.where(diag, value, 0.0).astype(BF)
-
-    for d in range(ND):
-        found = jnp.int32(0)
-        where = jnp.int32(0)
-        for t in range(mats.shape[0]):
-            hit = offsets[t] == d - REACH
-            found = jnp.where(hit, 1, found)
-            where = jnp.where(hit, t, where)
-        shifts[d] = (mats[where].astype(F32) * found.astype(F32)).astype(BF)
-
-    @pl.when(tile == 0)
-    def _():
-        coef_v[:, 0:PAD, :] = jnp.zeros((S, PAD, K), F32)
-
-    @pl.when(tile == last)
-    def _():
-        coef_v[:, NB + PAD : NB + 2 * PAD, :] = jnp.zeros((S, PAD, K), F32)
-
+    def halves(t):
+        for h in range(TB // HB):
+            b0 = pl.multiple_of(t * TB + h * HB, HB)
+            yield b0, pl.ds(b0, HB)
+
+    def weighted(boxes, cols, field):
+        adj = adj_v[:, boxes, cols].astype(F32)
+        return jnp.sum(adj * field.reshape(S, HB, CW), axis=0)
+
+    def encode(j, carry):
+        t = tile_at(j)
+        inc_copy(t).wait()
+        adj_copy(t).wait()
+        for b0, boxes in halves(t):
+            for c in range(NC):
+                cols = pl.ds(c * CW, CW)
+                enc = mm(enc_points[...], inc_v[:, boxes, cols].reshape(ROWS, CW))
+                first_v[boxes, cols] = weighted(boxes, cols, enc)
+        return carry
+
+    lax.fori_loop(0, NT, encode, 0)
     con_copy.wait()
 
     def project(t):
-        inc_copy(t).wait()
         for k in range(1, NG):
             ag_copy(t, k).wait_recv()
-        for h in range(TB // HB):
-            b0 = pl.multiple_of(t * TB + h * HB, HB)
-            boxes = pl.ds(b0, HB)
-            acc = jnp.zeros((S * HB, K), F32)
+        sums = []
+        for b0, boxes in halves(t):
+            acc = jnp.zeros((ROWS, K), F32)
             for c in range(NC):
                 cols = pl.ds(c * CW, CW)
-                enc = jnp.dot(
-                    kron[...],
-                    inc_v[:, boxes, cols].reshape(S * HB, CW),
-                    preferred_element_type=F32,
-                ).astype(BF).reshape(S, HB, CW)
-                enc_v[:, boxes, cols] = enc
-                src = enc * con_v[boxes, cols][None]
-                acc = acc + jnp.dot(
-                    src.reshape(S * HB, CW), proj[cols, :], preferred_element_type=F32
-                )
-            coef_v[:, pl.ds(pl.multiple_of(b0 + PAD, PAD), HB), :] = acc.reshape(S, HB, K)
+                src = inc_v[:, boxes, cols] * con_v[boxes, cols][None]
+                acc = acc + mm(src.reshape(ROWS, CW), proj[cols, :])
+            sums.append(acc.astype(BF))
+        for (b0, boxes), acc in zip(halves(t), sums):
+            coef = mm(enc_coeffs[...], acc).astype(BF)
+            coef_v[pl.ds(b0 + REACH, HB)] = coef.reshape(HB, S, K)
 
     def expand_terms(t):
-        adj_copy(t).wait()
-        for h in range(TB // HB):
-            b0 = pl.multiple_of(t * TB + h * HB, HB)
-            boxes = pl.ds(b0, HB)
-            acc = jnp.zeros((S * HB, K), F32)
-            window = coef_v.at[:, pl.ds(b0, HB + 2 * PAD), :]
-            for d in range(ND):
-                first = PAD + d - REACH
-                moved = window[:, first : first + HB, :]
-                acc = acc + jnp.dot(
-                    moved.astype(BF).reshape(S * HB, K), shifts[d], preferred_element_type=F32
-                )
-            local = acc.astype(BF)
+        sums = []
+        for b0, boxes in halves(t):
+            acc = jnp.zeros((ROWS, K), F32)
+            for i in range(mats.shape[0]):
+                moved = coef_v[pl.ds(b0 + REACH + offsets[i], HB)]
+                acc = acc + mm(moved.reshape(ROWS, K), mats[i])
+            sums.append(acc.astype(BF))
+        locals_ = [mm(perm[...], acc).astype(BF) for acc in sums]
+        for (b0, boxes), local in zip(halves(t), locals_):
             loc_v[:, boxes, :] = local.reshape(S, HB, K)
             for c in range(NC):
                 cols = pl.ds(c * CW, CW)
-                field = jnp.dot(local, expand[:, cols], preferred_element_type=F32)
-                total = enc_v[:, boxes, cols].astype(F32) + field.reshape(S, HB, CW)
-                term = jnp.sum(adj_v[:, boxes, cols].astype(F32) * total, axis=0).astype(BF)
+                field = mm(local, expand[:, cols])
+                term = (weighted(boxes, cols, field) + first_v[boxes, cols]).astype(BF)
                 for q in range(CW // GW):
                     term_v[c * (CW // GW) + q, boxes, :] = term[:, q * GW : (q + 1) * GW]
         loc_copy(t).start()
@@ -227,10 +227,20 @@
             @pl.when(tile > 0)
             def _():
                 halo_up().wait_recv()
+                coef_v[pl.ds(0, REACH)] = low_v[...]
+
+            @pl.when(tile == 0)
+            def _():
+                coef_v[pl.ds(0, REACH)] = jnp.zeros((REACH, S, K), BF)
 
             @pl.when(tile < last)
             def _():
                 halo_down().wait_recv()
+                coef_v[pl.ds(NB + REACH, REACH)] = high_v[...]
+
+            @pl.when(tile == last)
+            def _():
+                coef_v[pl.ds(NB + REACH, REACH)] = jnp.zeros((REACH, S, K), BF)
 
         @pl.when(j >= 3)
         def _():
@@ -265,9 +275,7 @@
     for c in range(NC):
         cols = pl.ds(c * CW, CW)
         scat[:, :, cols] = (
-            jnp.dot(loc[...].reshape(S * n, K), expand[:, cols], preferred_element_type=F32)
-            .astype(BF)
-            .reshape(S, n, CW)
+            mm(loc[...].reshape(S * n, K), expand[:, cols]).astype(BF).reshape(S, n, CW)
         )
     grad[...] = jnp.sum(part[...].astype(F32), axis=0)
 
@@ -289,12 +297,15 @@
             pltpu.VMEM((NB, PTS), BF),
             pltpu.VMEM((S, NB, PTS), BF),
             pltpu.VMEM((S, NB, PTS), BF),
-            pltpu.VMEM((S, NB, PTS), BF),
-            pltpu.VMEM((S, NB + 2 * PAD, K), F32),
+            pltpu.VMEM((NB + 2 * REACH, S, K), BF),
+            pltpu.VMEM((REACH, S, K), BF),
+            pltpu.VMEM((REACH, S, K), BF),
             pltpu.VMEM((S, NB, K), BF),
+            pltpu.VMEM((NB, PTS), F32),
             pltpu.VMEM((NG, NB, GW), BF),
-            pltpu.VMEM((S * HB, S * HB), BF),
-            pltpu.VMEM((ND, K, K), BF),
+            pltpu.VMEM((ROWS, ROWS), BF),
+            pltpu.VMEM((ROWS, ROWS), BF),
+            pltpu.VMEM((ROWS, ROWS), BF),
             dma((NT,)),
             dma,
             dma((NT,)),

time: 54.7 us -> 48.4 us (0.88)
  Pallas kernels: 53.7 us -> 47.5 us
    pallas_call x1, Pallas kernels: 44.9 us -> 38.7 us  [on_device(): pl.pallas_call(scatter_gradient_kernel, out_shape=(jax.ShapeDtypeStruct((...]
where the time goes in v2:
time: 48.4 us; the launch traced here: 48.1 us
  Pallas kernels  47.5 us (98%)
  between operations  0.64 us (1%)
    pallas_call x1, Pallas kernels, on_device(): pl.pallas_call(scatter_gradient_kernel, out_shape=(jax.ShapeDtypeStruct((...  38.7 us
    pallas_call x1, Pallas kernels, on_device(): pl.pallas_call(output_kernel, grid=(NT,), out_shape=(jax.ShapeDtypeStruct...  8.8 us

profile of v2, /device:TPU:0, one launch (start us, length us, event | category | flops | bytes accessed | tf_op | source)
XLA Modules:
  0.0 48.1 jit_solution(7444961416525718081)
XLA Ops:
  0.6 38.7 %shard_map.95 = (bf16[8,512,256]{2,1,0:T(8,128)(2,1)}, bf16[8,512,128]{2,1,0:T(8,128)(2,1)}) custom-call(s32[8,8]{1,0:T(8,128)} %bitcast.6, s32[6]{0:T(128)} %offsets.1, bf16[512,128]{1,0:T(8,128)(2,1)} %con_hbm.1, bf16[8,512,1024]{2,1,0:T(8,128)(2,1)} %bitcast.4, bf16[8,512,1024]{2,1,0:T(8,128)(2,1)} %bitcast.5, bf16[1024,256]{1,0:T(8,128)(2,1)} %proj.1, ...), custom_call_target="tpu_custom_call" | custom-call | tf_op jit(solution)/shard_map/pallas_call | solution.py:288
  39.3 8.8 %shard_map.96 = (bf16[8,512,1024]{2,1,0:T(8,128)(2,1)}, f32[512,128]{1,0:T(8,128)}) custom-call(bf16[8,512,256]{2,1,0:T(8,128)(2,1)} %get-tuple-element.6.loc, bf16[256,1024]{1,0:T(8,128)(2,1)} %expand.3, bf16[8,512,128]{2,1,0:T(8,128)(2,1)} %get-tuple-element.7.part), custom_call_target="tpu_custom_call" | custom-call | tf_op jit(solution)/shard_map/pallas_call | solution.py:326

commit v3 on v2

v3 whole, which is shorter than its diff:
```python
import jax
import jax.numpy as jnp
from jax import lax
from jax.experimental import pallas as pl
from jax.experimental.pallas import tpu as pltpu
from jax.sharding import PartitionSpec as P

MESH = pl.DeviceIdType.MESH
BF = jnp.bfloat16
F32 = jnp.float32

S = 8
K = 256
PTS = 1024
NB = 512
HB = 32
ROWS = S * HB
TB = 64
NT = NB // TB
NG = 8
GW = PTS // NG
CW = 256
NC = PTS // CW
REACH = 3
NZ = 4
CB = 128
NCH = NB // CB


def mm(a, b):
    return jnp.dot(a, b, preferred_element_type=F32)


def scatter_gradient_kernel(
    signs, offsets, con_hbm, inc_hbm, adj_hbm, proj, mats, expand,
    loc_hbm, part_hbm,
    con_v, inc_v, adj_v, coef_v, low_v, high_v, loc_v, first_v, term_v, stage_v, sum_v, own_v,
    enc_points, enc_coeffs, perm,
    in_sem, adj_sem, one_sem,
    ag_send, ag_recv, rs_send, rs_recv, halo_send, halo_recv,
):
    g = lax.axis_index("group")
    tile = lax.axis_index("tile")
    last = lax.axis_size("tile") - 1
    half = g // NZ
    z = lax.rem(g, NZ)
    partner = lax.rem(g + NZ, NG)

    def z_at(dz):
        return lax.rem(z + dz, NZ)

    def z_peer(dz):
        return half * NZ + z_at(dz)

    def rows_of(t):
        return pl.ds(pl.multiple_of(t * TB, TB), TB)

    def chunk_of(c):
        return pl.ds(pl.multiple_of(c * CB, CB), CB)

    def inc_copy(t):
        r = rows_of(t)
        return pltpu.make_async_copy(inc_hbm.at[:, r], inc_v.at[:, r], in_sem.at[t])

    def adj_copy(t):
        r = rows_of(t)
        return pltpu.make_async_copy(adj_hbm.at[:, r], adj_v.at[:, r], adj_sem.at[t])

    def remote(src, dst, send, recv, group, at=tile):
        return pltpu.make_async_remote_copy(
            src_ref=src,
            dst_ref=dst,
            send_sem=send,
            recv_sem=recv,
            device_id=(group, at),
            device_id_type=MESH,
        )

    con_copy = pltpu.make_async_copy(con_hbm, con_v.at[g], one_sem.at[0])
    own_copy = pltpu.make_async_copy(own_v, part_hbm.at[0], one_sem.at[1])
    loc_most = pl.ds(TB, NB - TB)
    loc_copies = [
        pltpu.make_async_copy(loc_v.at[:, r], loc_hbm.at[:, r], one_sem.at[2 + i])
        for i, r in enumerate((loc_most, pl.ds(0, TB)))
    ]

    def ag_direct(c, q):
        r = chunk_of(c)
        to = partner if q == 0 else z_peer(q)
        return remote(con_hbm.at[r], con_v.at[g, r], ag_send.at[c, q], ag_recv.at[c, q], to)

    def ag_relay(c, dz, even):
        r = chunk_of(c)
        held = con_v.at[partner if even else z_peer(NZ - dz), r]
        to = z_peer(dz) if even else partner
        return remote(held, held, ag_send.at[c, NZ - 1 + dz], ag_recv.at[c, NZ - 1 + dz], to)

    def gather_start(c):
        for q in range(NZ):
            ag_direct(c, q).start()

    def gather_pass(c, even):
        if even:
            ag_direct(c, 0).wait_recv()
        for dz in range(1, NZ):
            if not even:
                ag_direct(c, dz).wait_recv()
            ag_relay(c, dz, even).start()

    def gather_wait(c, even):
        for q in range(1, NZ) if even else (0,):
            ag_direct(c, q).wait_recv()
        for dz in range(1, NZ):
            ag_relay(c, dz, even).wait_recv()

    def z_terms(t, dz):
        r = rows_of(t)
        dst = stage_v.at[pl.ds(2 * (dz - 1), 2), r]
        return remote(term_v.at[z_at(dz), :, r], dst, rs_send.at[t, dz], rs_recv.at[t, dz], z_peer(dz))

    def z_sums(t):
        r = rows_of(t)
        return remote(sum_v.at[0, r], part_hbm.at[1, r], rs_send.at[t, 0], rs_recv.at[t, 0], partner)

    def half_terms(t):
        r = rows_of(t)
        dst = stage_v.at[pl.ds(0, NZ), r]
        return remote(term_v.at[:, 1 - half, r], dst, rs_send.at[t, 0], rs_recv.at[t, 0], partner)

    def half_sums(t, dz):
        r = rows_of(t)
        return remote(
            sum_v.at[z_at(dz), r], part_hbm.at[dz, r], rs_send.at[t, dz], rs_recv.at[t, dz], z_peer(dz)
        )

    def terms_start(t):
        even = lax.rem(t, 2) == 0

        @pl.when(even)
        def _():
            for dz in range(1, NZ):
                z_terms(t, dz).start()

        @pl.when(jnp.logical_not(even))
        def _():
            half_terms(t).start()

    def terms_pass(t):
        even = lax.rem(t, 2) == 0
        r = rows_of(t)

        @pl.when(even)
        def _():
            for dz in range(1, NZ):
                z_terms(t, dz).wait_recv()
            for h, out in ((half, own_v), (1 - half, sum_v.at[0])):
                total = term_v[z, h, r].astype(F32)
                for i in range(NZ - 1):
                    total = total + stage_v[2 * i + h, r].astype(F32)
                out[r] = total.astype(BF)
            z_sums(t).start()

        @pl.when(jnp.logical_not(even))
        def _():
            half_terms(t).wait_recv()
            for dz in range(NZ):
                to = z_at(dz)
                total = (term_v[to, half, r].astype(F32) + stage_v[to, r].astype(F32)).astype(BF)
                if dz == 0:
                    own_v[r] = total
                else:
                    sum_v[to, r] = total
            for dz in range(1, NZ):
                half_sums(t, dz).start()

    def halo_up():
        return remote(coef_v.at[pl.ds(NB, REACH)], low_v, halo_send.at[0], halo_recv.at[0], g, tile + 1)

    def halo_down():
        return remote(coef_v.at[pl.ds(REACH, REACH)], high_v, halo_send.at[1], halo_recv.at[1], g, tile - 1)

    for t in range(NT):
        inc_copy(t).start()
        adj_copy(t).start()
    con_copy.start()

    barrier = pltpu.get_barrier_semaphore()
    for to in [partner] + [z_peer(dz) for dz in range(1, NZ)]:
        pl.semaphore_signal(barrier, inc=1, device_id=(to, tile), device_id_type=MESH)
    for step_of in (1, last):
        pl.semaphore_signal(
            barrier, inc=1, device_id=(g, lax.rem(tile + step_of, last + 1)), device_id_type=MESH
        )

    lane8 = lax.broadcasted_iota(jnp.int32, (S, ROWS), 1)
    row8 = lax.broadcasted_iota(jnp.int32, (S, ROWS), 0)
    sign = jnp.zeros((S, ROWS), F32)
    for e in range(S):
        for s in range(S):
            here = (row8 == e) & (lane8 // HB == s)
            sign = jnp.where(here, signs[e, s].astype(F32), sign)
    for b in range(0, HB, 2):
        pair = [jnp.where(lax.rem(lane8, HB) == b + i, sign, 0.0) for i in range(2)]
        enc_coeffs[pl.ds(b * S, 2 * S), :] = jnp.concatenate(pair, axis=0).astype(BF)
    lane = lax.broadcasted_iota(jnp.int32, (HB, ROWS), 1)
    row = lax.broadcasted_iota(jnp.int32, (HB, ROWS), 0)
    for e in range(S):
        wide = jnp.broadcast_to(sign[e : e + 1, :], (HB, ROWS))
        enc_points[pl.ds(e * HB, HB), :] = jnp.where(lax.rem(lane, HB) == row, wide, 0.0).astype(BF)
        there = (lane // S == row) & (lax.rem(lane, S) == e)
        perm[pl.ds(e * HB, HB), :] = jnp.where(there, 1.0, 0.0).astype(BF)

    pl.semaphore_wait(barrier, NZ + 2)
    gather_start(0)
    gather_start(1)

    def halves(t):
        for h in range(TB // HB):
            b0 = pl.multiple_of(t * TB + h * HB, HB)
            yield b0, pl.ds(b0, HB)

    def weighted(boxes, cols, field):
        adj = adj_v[:, boxes, cols].astype(F32)
        return jnp.sum(adj * field.reshape(S, HB, CW), axis=0)

    def encode(t, carry):
        inc_copy(t).wait()
        adj_copy(t).wait()
        for b0, boxes in halves(t):
            for c in range(NC):
                cols = pl.ds(c * CW, CW)
                enc = mm(enc_points[...], inc_v[:, boxes, cols].reshape(ROWS, CW))
                first_v[boxes, cols] = weighted(boxes, cols, enc)

        @pl.when(t == NT - 2)
        def _():
            gather_pass(0, True)
            gather_start(2)

        return carry

    lax.fori_loop(0, NT, encode, 0)
    con_copy.wait()
    gather_pass(1, False)
    gather_start(3)

    def project(t):
        sums = []
        for b0, boxes in halves(t):
            acc = jnp.zeros((ROWS, K), F32)
            for c in range(NC):
                cols = pl.ds(c * CW, CW)
                pieces = [con_v[c * (CW // GW) + q, boxes] for q in range(CW // GW)]
                src = inc_v[:, boxes, cols] * jnp.concatenate(pieces, axis=1)[None]
                acc = acc + mm(src.reshape(ROWS, CW), proj[cols, :])
            sums.append(acc.astype(BF))
        for (b0, boxes), acc in zip(halves(t), sums):
            coef = mm(enc_coeffs[...], acc).astype(BF)
            coef_v[pl.ds(b0 + REACH, HB)] = coef.reshape(HB, S, K)

    def expand_terms(t):
        sums = []
        for b0, boxes in halves(t):
            acc = jnp.zeros((ROWS, K), F32)
            for i in range(mats.shape[0]):
                moved = coef_v[pl.ds(b0 + REACH + offsets[i], HB)]
                acc = acc + mm(moved.reshape(ROWS, K), mats[i])
            sums.append(acc.astype(BF))
        locals_ = [mm(perm[...], acc).astype(BF) for acc in sums]
        for (b0, boxes), local in zip(halves(t), locals_):
            loc_v[:, boxes, :] = local.reshape(S, HB, K)
            for c in range(NC):
                cols = pl.ds(c * CW, CW)
                field = mm(local, expand[:, cols])
                term = (weighted(boxes, cols, field) + first_v[boxes, cols]).astype(BF)
                for q in range(CW // GW):
                    h, to = divmod(c * (CW // GW) + q, NZ)
                    term_v[to, h, boxes, :] = term[:, q * GW : (q + 1) * GW]

    def step(j, carry):
        for c in range(NCH):

            @pl.when(j == c * (CB // TB))
            def _():
                gather_wait(c, c % 2 == 0)

        @pl.when(j < NT)
        def _():
            project(j)

        for c in range(2, NCH):

            @pl.when(j == c - 1)
            def _():
                gather_pass(c, c % 2 == 0)

        @pl.when(j == 1)
        def _():
            @pl.when(tile > 0)
            def _():
                halo_down().start()

        @pl.when(j == NT - 1)
        def _():
            @pl.when(tile < last)
            def _():
                halo_up().start()

        @pl.when(j == NT)
        def _():
            @pl.when(tile < last)
            def _():
                halo_down().wait_recv()
                coef_v[pl.ds(NB + REACH, REACH)] = high_v[...]

            @pl.when(tile == last)
            def _():
                coef_v[pl.ds(NB + REACH, REACH)] = jnp.zeros((REACH, S, K), BF)

        @pl.when(j == NT + 1)
        def _():
            loc_copies[0].start()

            @pl.when(tile > 0)
            def _():
                halo_up().wait_recv()
                coef_v[pl.ds(0, REACH)] = low_v[...]

            @pl.when(tile == 0)
            def _():
                coef_v[pl.ds(0, REACH)] = jnp.zeros((REACH, S, K), BF)

        @pl.when((j >= 2) & (j <= NT + 1))
        def _():
            t = jnp.where(j == NT + 1, 0, j - 1)
            expand_terms(t)
            terms_start(t)

        @pl.when(j == NT + 1)
        def _():
            loc_copies[1].start()

        @pl.when(j >= 4)
        def _():
            terms_pass(jnp.where(j == NT + 3, 0, j - 3))

        return carry

    lax.fori_loop(0, NT + 4, step, 0)
    own_copy.start()

    for c in range(NCH):
        for q in range(NZ):
            ag_direct(c, q).wait_send()
        for dz in range(1, NZ):
            ag_relay(c, dz, c % 2 == 0).wait_send()

    def finish(t, carry):
        even = lax.rem(t, 2) == 0

        @pl.when(even)
        def _():
            for dz in range(1, NZ):
                z_terms(t, dz).wait_send()
            z_sums(t).wait()

        @pl.when(jnp.logical_not(even))
        def _():
            half_terms(t).wait_send()
            for dz in range(1, NZ):
                half_sums(t, dz).wait()

        return carry

    lax.fori_loop(0, NT, finish, 0)
    for copy in loc_copies:
        copy.wait()
    own_copy.wait()

    @pl.when(tile < last)
    def _():
        halo_up().wait_send()

    @pl.when(tile > 0)
    def _():
        halo_down().wait_send()


def output_kernel(loc, expand, part, scat, grad):
    n = loc.shape[1]
    for c in range(NC):
        cols = pl.ds(c * CW, CW)
        scat[:, :, cols] = (
            mm(loc[...].reshape(S * n, K), expand[:, cols]).astype(BF).reshape(S, n, CW)
        )
    even = lax.rem(pl.program_id(0), 2) == 0

    @pl.when(even)
    def _():
        grad[...] = part[0].astype(F32) + part[1].astype(F32)

    @pl.when(jnp.logical_not(even))
    def _():
        grad[...] = jnp.sum(part[...].astype(F32), axis=0)


def on_device(contrast, incident, signs, adjoint, proj, mats, offsets, expand):
    any_spec = pl.BlockSpec(memory_space=pl.ANY)
    vmem = pl.BlockSpec(memory_space=pltpu.VMEM)
    smem = pl.BlockSpec(memory_space=pltpu.SMEM)
    dma = pltpu.SemaphoreType.DMA
    local, parts = pl.pallas_call(
        scatter_gradient_kernel,
        out_shape=(
            jax.ShapeDtypeStruct((S, NB, K), BF),
            jax.ShapeDtypeStruct((NZ, NB, GW), BF),
        ),
        in_specs=[smem, smem, any_spec, any_spec, any_spec, vmem, vmem, vmem],
        out_specs=(any_spec, any_spec),
        scratch_shapes=[
            pltpu.VMEM((NG, NB, GW), BF),
            pltpu.VMEM((S, NB, PTS), BF),
            pltpu.VMEM((S, NB, PTS), BF),
            pltpu.VMEM((NB + 2 * REACH, S, K), BF),
            pltpu.VMEM((REACH, S, K), BF),
            pltpu.VMEM((REACH, S, K), BF),
            pltpu.VMEM((S, NB, K), BF),
            pltpu.VMEM((NB, PTS), F32),
            pltpu.VMEM((NZ, 2, NB, GW), BF),
            pltpu.VMEM((2 * (NZ - 1), NB, GW), BF),
            pltpu.VMEM((NZ, NB, GW), BF),
            pltpu.VMEM((NB, GW), BF),
            pltpu.VMEM((ROWS, ROWS), BF),
            pltpu.VMEM((ROWS, ROWS), BF),
            pltpu.VMEM((ROWS, ROWS), BF),
            dma((NT,)),
            dma((NT,)),
            dma((4,)),
            dma((NCH, 2 * NZ - 1)),
            dma((NCH, 2 * NZ - 1)),
            dma((NT, NZ)),
            dma((NT, NZ)),
            dma((2,)),
            dma((2,)),
        ],
        compiler_params=pltpu.CompilerParams(
            collective_id=0, has_side_effects=True, vmem_limit_bytes=60 << 20
        ),
    )(signs[0], offsets, contrast, incident[0], adjoint[0], proj, mats, expand)

    scattered, gradient = pl.pallas_call(
        output_kernel,
        grid=(NT,),
        out_shape=(
            jax.ShapeDtypeStruct((S, NB, PTS), BF),
            jax.ShapeDtypeStruct((NB, GW), F32),
        ),
        in_specs=[
            pl.BlockSpec((S, TB, K), lambda i: (0, i, 0)),
            pl.BlockSpec((K, PTS), lambda i: (0, 0)),
            pl.BlockSpec((NZ, TB, GW), lambda i: (0, i, 0)),
        ],
        out_specs=(
            pl.BlockSpec((S, TB, PTS), lambda i: (0, i, 0)),
            pl.BlockSpec((TB, GW), lambda i: (i, 0)),
        ),
        compiler_params=pltpu.CompilerParams(vmem_limit_bytes=60 << 20),
    )(local, expand, parts)
    return scattered[None], gradient


def solution(mesh):
    in_specs = (
        P("tile", "group"),
        P("group", None, "tile", None),
        P("group", None, None),
        P("group", None, "tile", None),
        P(),
        P(),
        P(),
        P(),
    )
    out_specs = (P("group", None, "tile", None), P("tile", "group"))
    return jax.shard_map(
        on_device, mesh=mesh, in_specs=in_specs, out_specs=out_specs, check_vma=False
    )
```

time: 48.4 us -> 51.5 us (1.064)
  Pallas kernels: 47.5 us -> 50.6 us
    pallas_call x1, Pallas kernels: 38.7 us -> 42.1 us  [on_device(): pl.pallas_call(scatter_gradient_kernel, out_shape=(jax.ShapeDtypeStruct((...]
where the time goes in v3:
time: 51.5 us; the launch traced here: 51.2 us
  Pallas kernels  50.6 us (98%)
  between operations  0.64 us (1%)
    pallas_call x1, Pallas kernels, on_device(): pl.pallas_call(scatter_gradient_kernel, out_shape=(jax.ShapeDtypeStruct((...  42.1 us
    pallas_call x1, Pallas kernels, on_device(): pl.pallas_call(output_kernel, grid=(NT,), out_shape=(jax.ShapeDtypeStruct...  8.54 us

profile of v3, /device:TPU:0, one launch (start us, length us, event | category | flops | bytes accessed | tf_op | source)
XLA Modules:
  0.0 51.2 jit_solution(14600659201102989309)
XLA Ops:
  0.6 42.1 %shard_map.95 = (bf16[8,512,256]{2,1,0:T(8,128)(2,1)}, bf16[4,512,128]{2,1,0:T(8,128)(2,1)}) custom-call(s32[8,8]{1,0:T(8,128)} %bitcast.6, s32[6]{0:T(128)} %offsets.1, bf16[512,128]{1,0:T(8,128)(2,1)} %con_hbm.1, bf16[8,512,1024]{2,1,0:T(8,128)(2,1)} %bitcast.4, bf16[8,512,1024]{2,1,0:T(8,128)(2,1)} %bitcast.5, bf16[1024,256]{1,0:T(8,128)(2,1)} %proj.1, ...), custom_call_target="tpu_custom_call" | custom-call | tf_op jit(solution)/shard_map/pallas_call | solution.py:412
  42.7 8.5 %shard_map.96 = (bf16[8,512,1024]{2,1,0:T(8,128)(2,1)}, f32[512,128]{1,0:T(8,128)}) custom-call(bf16[8,512,256]{2,1,0:T(8,128)(2,1)} %get-tuple-element.6.loc, bf16[256,1024]{1,0:T(8,128)(2,1)} %expand.3, bf16[4,512,128]{2,1,0:T(8,128)(2,1)} %get-tuple-element.7.part), custom_call_target="tpu_custom_call" | custom-call | tf_op jit(solution)/shard_map/pallas_call | solution.py:451

commit v4 on v2

--- a/solution.py
+++ b/solution.py
@@ -22,17 +22,24 @@
 CW = 256
 NC = PTS // CW
 REACH = 3
+NZ = 4
+ET = 2
 
 
 def mm(a, b):
     return jnp.dot(a, b, preferred_element_type=F32)
 
 
+def wait_bytes(ref, sem):
+    pltpu.make_async_copy(ref, ref, sem).wait()
+
+
 def scatter_gradient_kernel(
-    signs, offsets, con_hbm, inc_hbm, adj_hbm, proj, mats, expand,
+    signs_hbm, offsets_hbm, con_hbm, inc_hbm, adj_hbm, proj_hbm, mats_hbm, expand_hbm,
     loc_hbm, part_hbm,
+    signs, offsets, proj, mats, expand,
     con_v, inc_v, adj_v, coef_v, low_v, high_v, loc_v, first_v, term_v, enc_points, enc_coeffs, perm,
-    in_sem, con_sem, adj_sem, loc_sem, own_sem,
+    small_sem, in_sem, adj_sem, con_sem, loc_sem, own_sem,
     ag_send, ag_recv, rs_send, rs_recv, halo_send, halo_recv,
 ):
     g = lax.axis_index("group")
@@ -50,15 +57,27 @@
         r = rows_of(t)
         return pltpu.make_async_copy(adj_hbm.at[:, r], adj_v.at[:, r], adj_sem.at[t])
 
-    mine = pl.ds(pl.multiple_of(g * GW, GW), GW)
-    con_copy = pltpu.make_async_copy(con_hbm, con_v.at[:, mine], con_sem)
-
-    def ag_copy(t, k):
+    con_copy = pltpu.make_async_copy(con_hbm, con_v.at[g], con_sem)
+    small_copies = [
+        pltpu.make_async_copy(src, dst, small_sem.at[i])
+        for i, (src, dst) in enumerate(
+            (
+                (signs_hbm, signs),
+                (offsets_hbm, offsets),
+                (proj_hbm, proj),
+                (mats_hbm, mats),
+                (expand_hbm, expand),
+            )
+        )
+    ]
+
+    def gather(t, k):
+        r = rows_of(t)
         return pltpu.make_async_remote_copy(
-            src_ref=con_hbm.at[rows_of(t)],
-            dst_ref=con_v.at[rows_of(t), mine],
-            send_sem=ag_send.at[t, k - 1],
-            recv_sem=ag_recv.at[t, k - 1],
+            src_ref=con_hbm.at[r],
+            dst_ref=con_v.at[g, r],
+            send_sem=ag_send,
+            recv_sem=ag_recv.at[t],
             device_id=(lax.rem(g + k, NG), tile),
             device_id_type=MESH,
         )
@@ -68,19 +87,19 @@
         return pltpu.make_async_remote_copy(
             src_ref=term_v.at[peer, rows_of(t)],
             dst_ref=part_hbm.at[g, rows_of(t)],
-            send_sem=rs_send.at[t, k - 1],
-            recv_sem=rs_recv.at[t, k - 1],
+            send_sem=rs_send,
+            recv_sem=rs_recv,
             device_id=(peer, tile),
             device_id_type=MESH,
         )
 
     def own_copy(t):
         r = rows_of(t)
-        return pltpu.make_async_copy(term_v.at[g, r], part_hbm.at[g, r], own_sem.at[t])
+        return pltpu.make_async_copy(term_v.at[g, r], part_hbm.at[g, r], own_sem)
 
     def loc_copy(t):
         r = rows_of(t)
-        return pltpu.make_async_copy(loc_v.at[:, r], loc_hbm.at[:, r], loc_sem.at[t])
+        return pltpu.make_async_copy(loc_v.at[:, r], loc_hbm.at[:, r], loc_sem)
 
     def halo_up():
         return pltpu.make_async_remote_copy(
@@ -102,14 +121,6 @@
             device_id_type=MESH,
         )
 
-    def tile_at(j):
-        return jnp.where(j == 0, 0, jnp.where(j == 1, NT - 1, j - 1))
-
-    con_copy.start()
-    for t in [0, NT - 1] + list(range(1, NT - 1)):
-        inc_copy(t).start()
-        adj_copy(t).start()
-
     barrier = pltpu.get_barrier_semaphore()
     for k in range(1, NG):
         pl.semaphore_signal(
@@ -119,6 +130,18 @@
         pl.semaphore_signal(
             barrier, inc=1, device_id=(g, lax.rem(tile + step_of, last + 1)), device_id_type=MESH
         )
+
+    small_copies[0].start()
+    small_copies[1].start()
+    for t in range(NT):
+        inc_copy(t).start()
+        adj_copy(t).start()
+        if t == 1:
+            con_copy.start()
+            for copy in small_copies[2:]:
+                copy.start()
+    small_copies[0].wait()
+    small_copies[1].wait()
 
     lane8 = lax.broadcasted_iota(jnp.int32, (S, ROWS), 1)
     row8 = lax.broadcasted_iota(jnp.int32, (S, ROWS), 0)
@@ -138,17 +161,8 @@
         there = (lane // S == row) & (lax.rem(lane, S) == e)
         perm[pl.ds(e * HB, HB), :] = jnp.where(there, 1.0, 0.0).astype(BF)
 
-    pl.semaphore_wait(barrier, NG + 1)
-
-    def ag_start(j, carry):
-        for k in range(1, NG):
-            ag_copy(tile_at(j), k).start()
-        return carry
-
-    lax.fori_loop(0, NT, ag_start, 0)
-
-    def halves(t):
-        for h in range(TB // HB):
+    def halves(t, tiles=1):
+        for h in range(tiles * TB // HB):
             b0 = pl.multiple_of(t * TB + h * HB, HB)
             yield b0, pl.ds(b0, HB)
 
@@ -156,29 +170,39 @@
         adj = adj_v[:, boxes, cols].astype(F32)
         return jnp.sum(adj * field.reshape(S, HB, CW), axis=0)
 
-    def encode(j, carry):
-        t = tile_at(j)
-        inc_copy(t).wait()
-        adj_copy(t).wait()
-        for b0, boxes in halves(t):
+    early = (2 * NZ - 1 - lax.rem(g, NZ) - NZ + (1 - g // NZ)) // 2
+
+    def encode(i, carry):
+        @pl.when(i == early)
+        def _():
+            pl.semaphore_wait(barrier, NG + 1)
+            for t in range(NT):
+                for k in range(1, NG):
+                    gather(t, k).start()
+
+        for t in range(ET):
+            inc_copy(ET * i + t).wait()
+            adj_copy(ET * i + t).wait()
+        for b0, boxes in halves(ET * i, ET):
             for c in range(NC):
                 cols = pl.ds(c * CW, CW)
                 enc = mm(enc_points[...], inc_v[:, boxes, cols].reshape(ROWS, CW))
                 first_v[boxes, cols] = weighted(boxes, cols, enc)
         return carry
 
-    lax.fori_loop(0, NT, encode, 0)
+    lax.fori_loop(0, NT // ET, encode, 0)
     con_copy.wait()
+    for copy in small_copies[2:]:
+        copy.wait()
 
     def project(t):
-        for k in range(1, NG):
-            ag_copy(t, k).wait_recv()
         sums = []
         for b0, boxes in halves(t):
             acc = jnp.zeros((ROWS, K), F32)
             for c in range(NC):
                 cols = pl.ds(c * CW, CW)
-                src = inc_v[:, boxes, cols] * con_v[boxes, cols][None]
+                pieces = [con_v[c * (CW // GW) + q, boxes] for q in range(CW // GW)]
+                src = inc_v[:, boxes, cols] * jnp.concatenate(pieces, axis=1)[None]
                 acc = acc + mm(src.reshape(ROWS, CW), proj[cols, :])
             sums.append(acc.astype(BF))
         for (b0, boxes), acc in zip(halves(t), sums):
@@ -210,17 +234,27 @@
     def step(j, carry):
         @pl.when(j < NT)
         def _():
-            project(tile_at(j))
-
-        @pl.when(j == 2)
+            wait_bytes(con_v.at[pl.ds(0, NG - 1), pl.ds(0, TB)], ag_recv.at[j])
+            project(j)
+
+        @pl.when((j == 1) & (tile > 0))
+        def _():
+            halo_down().start()
+
+        @pl.when((j == NT - 1) & (tile < last))
+        def _():
+            halo_up().start()
+
+        @pl.when(j == NT)
         def _():
             @pl.when(tile < last)
             def _():
-                halo_up().start()
-
-            @pl.when(tile > 0)
+                halo_down().wait_recv()
+                coef_v[pl.ds(NB + REACH, REACH)] = high_v[...]
+
+            @pl.when(tile == last)
             def _():
-                halo_down().start()
+                coef_v[pl.ds(NB + REACH, REACH)] = jnp.zeros((REACH, S, K), BF)
 
         @pl.when(j == NT + 1)
         def _():
@@ -233,33 +267,19 @@
             def _():
                 coef_v[pl.ds(0, REACH)] = jnp.zeros((REACH, S, K), BF)
 
-            @pl.when(tile < last)
-            def _():
-                halo_down().wait_recv()
-                coef_v[pl.ds(NB + REACH, REACH)] = high_v[...]
-
-            @pl.when(tile == last)
-            def _():
-                coef_v[pl.ds(NB + REACH, REACH)] = jnp.zeros((REACH, S, K), BF)
-
-        @pl.when(j >= 3)
-        def _():
-            expand_terms(jnp.where(j == NT + 1, 0, jnp.where(j == NT + 2, NT - 1, j - 2)))
+        @pl.when(j >= 2)
+        def _():
+            expand_terms(jnp.where(j == NT + 1, 0, j - 1))
 
         return carry
 
-    lax.fori_loop(0, NT + 3, step, 0)
-
-    def finish(t, carry):
-        loc_copy(t).wait()
-        own_copy(t).wait()
-        for k in range(1, NG):
-            ag_copy(t, k).wait_send()
-            rs_copy(t, k).wait_send()
-            rs_copy(t, k).wait_recv()
-        return carry
-
-    lax.fori_loop(0, NT, finish, 0)
+    lax.fori_loop(0, NT + 2, step, 0)
+
+    wait_bytes(loc_v, loc_sem)
+    wait_bytes(term_v.at[0], own_sem)
+    wait_bytes(con_v.at[pl.ds(0, NG - 1)], ag_send)
+    wait_bytes(term_v.at[pl.ds(0, NG - 1)], rs_send)
+    wait_bytes(part_hbm.at[pl.ds(0, NG - 1)], rs_recv)
 
     @pl.when(tile < last)
     def _():
@@ -270,20 +290,56 @@
         halo_down().wait_send()
 
 
-def output_kernel(loc, expand, part, scat, grad):
-    n = loc.shape[1]
-    for c in range(NC):
-        cols = pl.ds(c * CW, CW)
-        scat[:, :, cols] = (
-            mm(loc[...].reshape(S * n, K), expand[:, cols]).astype(BF).reshape(S, n, CW)
-        )
-    grad[...] = jnp.sum(part[...].astype(F32), axis=0)
+def output_kernel(
+    loc_hbm, expand_hbm, part_hbm, scat_hbm, grad_hbm,
+    loc_v, expand, part_v, scat_v, grad_v, loc_sem, expand_sem, part_sem, scat_sem, grad_sem,
+):
+    def rows_of(t):
+        return pl.ds(pl.multiple_of(t * TB, TB), TB)
+
+    def loc_copy(t):
+        r = rows_of(t)
+        return pltpu.make_async_copy(loc_hbm.at[:, r], loc_v.at[:, r], loc_sem.at[t])
+
+    def scat_copy(t, e):
+        r = rows_of(t)
+        return pltpu.make_async_copy(scat_v.at[e, r], scat_hbm.at[e, r], scat_sem)
+
+    expand_copy = pltpu.make_async_copy(expand_hbm, expand, expand_sem)
+    part_copy = pltpu.make_async_copy(part_hbm, part_v, part_sem)
+    grad_copy = pltpu.make_async_copy(grad_v, grad_hbm, grad_sem)
+    loc_copy(0).start()
+    expand_copy.start()
+    for t in range(1, NT):
+        loc_copy(t).start()
+    part_copy.start()
+    expand_copy.wait()
+
+    def step(t, carry):
+        loc_copy(t).wait()
+        r = rows_of(t)
+        rows = loc_v[:, r, :].reshape(S * TB, K)
+        for c in range(NC):
+            cols = pl.ds(c * CW, CW)
+            scat_v[:, r, cols] = mm(rows, expand[:, cols]).astype(BF).reshape(S, TB, CW)
+        for e in range(S):
+            scat_copy(t, e).start()
+
+        @pl.when(t == NT - 2)
+        def _():
+            part_copy.wait()
+            grad_v[...] = jnp.sum(part_v[...].astype(F32), axis=0)
+            grad_copy.start()
+
+        return carry
+
+    lax.fori_loop(0, NT, step, 0)
+    wait_bytes(scat_v, scat_sem)
+    grad_copy.wait()
 
 
 def on_device(contrast, incident, signs, adjoint, proj, mats, offsets, expand):
     any_spec = pl.BlockSpec(memory_space=pl.ANY)
-    vmem = pl.BlockSpec(memory_space=pltpu.VMEM)
-    smem = pl.BlockSpec(memory_space=pltpu.SMEM)
     dma = pltpu.SemaphoreType.DMA
     local, parts = pl.pallas_call(
         scatter_gradient_kernel,
@@ -291,10 +347,15 @@
             jax.ShapeDtypeStruct((S, NB, K), BF),
             jax.ShapeDtypeStruct((NG, NB, GW), BF),
         ),
-        in_specs=[smem, smem, any_spec, any_spec, any_spec, vmem, vmem, vmem],
+        in_specs=[any_spec] * 8,
         out_specs=(any_spec, any_spec),
         scratch_shapes=[
-            pltpu.VMEM((NB, PTS), BF),
+            pltpu.SMEM((S, S), jnp.int32),
+            pltpu.SMEM(offsets.shape, jnp.int32),
+            pltpu.VMEM(proj.shape, BF),
+            pltpu.VMEM(mats.shape, BF),
+            pltpu.VMEM(expand.shape, BF),
+            pltpu.VMEM((NG, NB, GW), BF),
             pltpu.VMEM((S, NB, PTS), BF),
             pltpu.VMEM((S, NB, PTS), BF),
             pltpu.VMEM((NB + 2 * REACH, S, K), BF),
@@ -306,15 +367,16 @@
             pltpu.VMEM((ROWS, ROWS), BF),
             pltpu.VMEM((ROWS, ROWS), BF),
             pltpu.VMEM((ROWS, ROWS), BF),
-            dma((NT,)),
-            dma,
+            dma((5,)),
             dma((NT,)),
             dma((NT,)),
+            dma,
+            dma,
+            dma,
+            dma,
             dma((NT,)),
-            dma((NT, NG - 1)),
-            dma((NT, NG - 1)),
-            dma((NT, NG - 1)),
-            dma((NT, NG - 1)),
+            dma,
+            dma,
             dma((2,)),
             dma((2,)),
         ],
@@ -325,20 +387,24 @@
 
     scattered, gradient = pl.pallas_call(
         output_kernel,
-        grid=(NT,),
         out_shape=(
             jax.ShapeDtypeStruct((S, NB, PTS), BF),
             jax.ShapeDtypeStruct((NB, GW), F32),
         ),
-        in_specs=[
-            pl.BlockSpec((S, TB, K), lambda i: (0, i, 0)),
-            pl.BlockSpec((K, PTS), lambda i: (0, 0)),
-            pl.BlockSpec((NG, TB, GW), lambda i: (0, i, 0)),
+        in_specs=[any_spec] * 3,
+        out_specs=(any_spec, any_spec),
+        scratch_shapes=[
+            pltpu.VMEM((S, NB, K), BF),
+            pltpu.VMEM(expand.shape, BF),
+            pltpu.VMEM((NG, NB, GW), BF),
+            pltpu.VMEM((S, NB, PTS), BF),
+            pltpu.VMEM((NB, GW), F32),
+            dma((NT,)),
+            dma,
+            dma,
+            dma,
+            dma,
         ],
-        out_specs=(
-            pl.BlockSpec((S, TB, PTS), lambda i: (0, i, 0)),
-            pl.BlockSpec((TB, GW), lambda i: (i, 0)),
-        ),
         compiler_params=pltpu.CompilerParams(vmem_limit_bytes=60 << 20),
     )(local, expand, parts)
     return scattered[None], gradient

time: 48.4 us -> 41.5 us (0.86)
  Pallas kernels: 47.5 us -> 40.7 us
    pallas_call x1, Pallas kernels: 38.7 us -> 34.4 us  [on_device(): pl.pallas_call(scatter_gradient_kernel, out_shape=(jax.ShapeDtypeStruct((...]
    pallas_call x1, Pallas kernels: 8.8 us -> 6.36 us  [on_device(): pl.pallas_call(output_kernel, out_shape=(jax.ShapeDtypeStruct((S, NB, PTS...]
where the time goes in v4:
time: 41.5 us; the launch traced here: 41.4 us
  Pallas kernels  40.7 us (98%)
  between operations  0.64 us (2%)
    pallas_call x1, Pallas kernels, on_device(): pl.pallas_call(scatter_gradient_kernel, out_shape=(jax.ShapeDtypeStruct((...  34.4 us
    pallas_call x1, Pallas kernels, on_device(): pl.pallas_call(output_kernel, out_shape=(jax.ShapeDtypeStruct((S, NB, PTS...  6.36 us

profile of v4, /device:TPU:0, one launch (start us, length us, event | category | flops | bytes accessed | tf_op | source)
XLA Modules:
  0.0 41.4 jit_solution(2590879272273362533)
XLA Ops:
  0.6 34.4 %shard_map.95 = (bf16[8,512,256]{2,1,0:T(8,128)(2,1)}, bf16[8,512,128]{2,1,0:T(8,128)(2,1)}) custom-call(s32[8,8]{1,0:T(8,128)} %bitcast.6, s32[6]{0:T(128)} %offsets_hbm.1, bf16[512,128]{1,0:T(8,128)(2,1)} %con_hbm.1, bf16[8,512,1024]{2,1,0:T(8,128)(2,1)} %bitcast.4, bf16[8,512,1024]{2,1,0:T(8,128)(2,1)} %bitcast.5, bf16[1024,256]{1,0:T(8,128)(2,1)} %proj_hbm.1, ...), custom_call_target="tpu_custom_call" | custom-call | tf_op jit(solution)/shard_map/pallas_call | solution.py:344
  35.0 6.4 %shard_map.96 = (bf16[8,512,1024]{2,1,0:T(8,128)(2,1)}, f32[512,128]{1,0:T(8,128)}) custom-call(bf16[8,512,256]{2,1,0:T(8,128)(2,1)} %get-tuple-element.6.loc_hbm, bf16[256,1024]{1,0:T(8,128)(2,1)} %expand_hbm.3, bf16[8,512,128]{2,1,0:T(8,128)(2,1)} %get-tuple-element.7.part_hbm), custom_call_target="tpu_custom_call" | custom-call | tf_op jit(solution)/shard_map/pallas_call | solution.py:388

commit v5 on v4

--- a/solution.py
+++ b/solution.py
@@ -22,7 +22,9 @@
 CW = 256
 NC = PTS // CW
 REACH = 3
+LANES = 128
 NZ = 4
+PEERS = [(1, 2), (1, 1), (1, 3), (0, 2), (1, 0), (0, 1), (0, 3)]
 ET = 2
 
 
@@ -38,13 +40,20 @@
     signs_hbm, offsets_hbm, con_hbm, inc_hbm, adj_hbm, proj_hbm, mats_hbm, expand_hbm,
     loc_hbm, part_hbm,
     signs, offsets, proj, mats, expand,
-    con_v, inc_v, adj_v, coef_v, low_v, high_v, loc_v, first_v, term_v, enc_points, enc_coeffs, perm,
+    con_v, inc_v, adj_v, coef_v, low_v, high_v, loc_v, first_v, term_v, enc_points, enc_coeffs,
     small_sem, in_sem, adj_sem, con_sem, loc_sem, own_sem,
     ag_send, ag_recv, rs_send, rs_recv, halo_send, halo_recv,
 ):
     g = lax.axis_index("group")
     tile = lax.axis_index("tile")
     last = lax.axis_size("tile") - 1
+
+    flip = lax.rem(tile, 2)
+
+    def peer_at(k):
+        dy, dz = PEERS[k - 1]
+        step = dz + flip * ((NZ - 2 * dz) if dz else 0)
+        return lax.rem(g // NZ + dy, 2) * NZ + lax.rem(g + step, NZ)
 
     def rows_of(t):
         return pl.ds(pl.multiple_of(t * TB, TB), TB)
@@ -78,12 +87,12 @@
             dst_ref=con_v.at[g, r],
             send_sem=ag_send,
             recv_sem=ag_recv.at[t],
-            device_id=(lax.rem(g + k, NG), tile),
+            device_id=(peer_at(k), tile),
             device_id_type=MESH,
         )
 
     def rs_copy(t, k):
-        peer = lax.rem(g + k, NG)
+        peer = peer_at(k)
         return pltpu.make_async_remote_copy(
             src_ref=term_v.at[peer, rows_of(t)],
             dst_ref=part_hbm.at[g, rows_of(t)],
@@ -103,7 +112,7 @@
 
     def halo_up():
         return pltpu.make_async_remote_copy(
-            src_ref=coef_v.at[pl.ds(NB, REACH)],
+            src_ref=coef_v.at[:, pl.ds(NB * S, REACH * S)],
             dst_ref=low_v,
             send_sem=halo_send.at[0],
             recv_sem=halo_recv.at[0],
@@ -113,7 +122,7 @@
 
     def halo_down():
         return pltpu.make_async_remote_copy(
-            src_ref=coef_v.at[pl.ds(REACH, REACH)],
+            src_ref=coef_v.at[:, pl.ds(REACH * S, REACH * S)],
             dst_ref=high_v,
             send_sem=halo_send.at[1],
             recv_sem=halo_recv.at[1],
@@ -158,8 +167,6 @@
     for e in range(S):
         wide = jnp.broadcast_to(sign[e : e + 1, :], (HB, ROWS))
         enc_points[pl.ds(e * HB, HB), :] = jnp.where(lax.rem(lane, HB) == row, wide, 0.0).astype(BF)
-        there = (lane // S == row) & (lax.rem(lane, S) == e)
-        perm[pl.ds(e * HB, HB), :] = jnp.where(there, 1.0, 0.0).astype(BF)
 
     def halves(t, tiles=1):
         for h in range(tiles * TB // HB):
@@ -206,19 +213,26 @@
                 acc = acc + mm(src.reshape(ROWS, CW), proj[cols, :])
             sums.append(acc.astype(BF))
         for (b0, boxes), acc in zip(halves(t), sums):
-            coef = mm(enc_coeffs[...], acc).astype(BF)
-            coef_v[pl.ds(b0 + REACH, HB)] = coef.reshape(HB, S, K)
+            coef = mm(enc_coeffs[...], acc)
+            to = pl.ds(pl.multiple_of((b0 + REACH) * S, S), ROWS)
+            for w in range(K // LANES):
+                coef_v[w, to, :] = coef[:, w * LANES : (w + 1) * LANES]
 
     def expand_terms(t):
         sums = []
         for b0, boxes in halves(t):
             acc = jnp.zeros((ROWS, K), F32)
             for i in range(mats.shape[0]):
-                moved = coef_v[pl.ds(b0 + REACH + offsets[i], HB)]
-                acc = acc + mm(moved.reshape(ROWS, K), mats[i])
+                first = (b0 + REACH + offsets[i]) * S
+                moved = [
+                    jnp.concatenate(
+                        [coef_v[w, pl.ds(first + e, HB, stride=S), :] for e in range(S)], axis=0
+                    ).astype(BF)
+                    for w in range(K // LANES)
+                ]
+                acc = acc + mm(jnp.concatenate(moved, axis=1), mats[i])
             sums.append(acc.astype(BF))
-        locals_ = [mm(perm[...], acc).astype(BF) for acc in sums]
-        for (b0, boxes), local in zip(halves(t), locals_):
+        for (b0, boxes), local in zip(halves(t), sums):
             loc_v[:, boxes, :] = local.reshape(S, HB, K)
             for c in range(NC):
                 cols = pl.ds(c * CW, CW)
@@ -250,22 +264,22 @@
             @pl.when(tile < last)
             def _():
                 halo_down().wait_recv()
-                coef_v[pl.ds(NB + REACH, REACH)] = high_v[...]
+                coef_v[:, pl.ds((NB + REACH) * S, REACH * S)] = high_v[...]
 
             @pl.when(tile == last)
             def _():
-                coef_v[pl.ds(NB + REACH, REACH)] = jnp.zeros((REACH, S, K), BF)
+                coef_v[:, pl.ds((NB + REACH) * S, REACH * S)] = jnp.zeros((K // LANES, REACH * S, LANES), F32)
 
         @pl.when(j == NT + 1)
         def _():
             @pl.when(tile > 0)
             def _():
                 halo_up().wait_recv()
-                coef_v[pl.ds(0, REACH)] = low_v[...]
+                coef_v[:, pl.ds(0, REACH * S)] = low_v[...]
 
             @pl.when(tile == 0)
             def _():
-                coef_v[pl.ds(0, REACH)] = jnp.zeros((REACH, S, K), BF)
+                coef_v[:, pl.ds(0, REACH * S)] = jnp.zeros((K // LANES, REACH * S, LANES), F32)
 
         @pl.when(j >= 2)
         def _():
@@ -315,17 +329,21 @@
     part_copy.start()
     expand_copy.wait()
 
-    def step(t, carry):
-        loc_copy(t).wait()
-        r = rows_of(t)
-        rows = loc_v[:, r, :].reshape(S * TB, K)
-        for c in range(NC):
-            cols = pl.ds(c * CW, CW)
-            scat_v[:, r, cols] = mm(rows, expand[:, cols]).astype(BF).reshape(S, TB, CW)
-        for e in range(S):
-            scat_copy(t, e).start()
-
-        @pl.when(t == NT - 2)
+    def step(i, carry):
+        tiles = [ET * i + t for t in range(ET)]
+        for t in tiles:
+            loc_copy(t).wait()
+        for t in tiles:
+            r = rows_of(t)
+            rows = loc_v[:, r, :].reshape(S * TB, K)
+            for c in range(NC):
+                cols = pl.ds(c * CW, CW)
+                scat_v[:, r, cols] = mm(rows, expand[:, cols]).astype(BF).reshape(S, TB, CW)
+        for t in tiles:
+            for e in range(S):
+                scat_copy(t, e).start()
+
+        @pl.when(i == NT // ET - 2)
         def _():
             part_copy.wait()
             grad_v[...] = jnp.sum(part_v[...].astype(F32), axis=0)
@@ -333,7 +351,7 @@
 
         return carry
 
-    lax.fori_loop(0, NT, step, 0)
+    lax.fori_loop(0, NT // ET, step, 0)
     wait_bytes(scat_v, scat_sem)
     grad_copy.wait()
 
@@ -358,13 +376,12 @@
             pltpu.VMEM((NG, NB, GW), BF),
             pltpu.VMEM((S, NB, PTS), BF),
             pltpu.VMEM((S, NB, PTS), BF),
-            pltpu.VMEM((NB + 2 * REACH, S, K), BF),
-            pltpu.VMEM((REACH, S, K), BF),
-            pltpu.VMEM((REACH, S, K), BF),
+            pltpu.VMEM((K // LANES, (NB + 2 * REACH) * S, LANES), F32),
+            pltpu.VMEM((K // LANES, REACH * S, LANES), F32),
+            pltpu.VMEM((K // LANES, REACH * S, LANES), F32),
             pltpu.VMEM((S, NB, K), BF),
             pltpu.VMEM((NB, PTS), F32),
             pltpu.VMEM((NG, NB, GW), BF),
-            pltpu.VMEM((ROWS, ROWS), BF),
             pltpu.VMEM((ROWS, ROWS), BF),
             pltpu.VMEM((ROWS, ROWS), BF),
             dma((5,)),

time: 41.5 us -> 39.5 us (0.952)
  Pallas kernels: 40.7 us -> 38.8 us
    pallas_call x1, Pallas kernels: 34.4 us -> 32.8 us  [on_device(): pl.pallas_call(scatter_gradient_kernel, out_shape=(jax.ShapeDtypeStruct((...]
where the time goes in v5:
time: 39.5 us; the launch traced here: 39.4 us
  Pallas kernels  38.8 us (98%)
  between operations  0.64 us (2%)
    pallas_call x1, Pallas kernels, on_device(): pl.pallas_call(scatter_gradient_kernel, out_shape=(jax.ShapeDtypeStruct((...  32.8 us
    pallas_call x1, Pallas kernels, on_device(): pl.pallas_call(output_kernel, out_shape=(jax.ShapeDtypeStruct((S, NB, PTS...  5.99 us

profile of v5, /device:TPU:0, one launch (start us, length us, event | category | flops | bytes accessed | tf_op | source)
XLA Modules:
  0.0 39.4 jit_solution(17134265590446935767)
XLA Ops:
  0.6 32.8 %shard_map.95 = (bf16[8,512,256]{2,1,0:T(8,128)(2,1)}, bf16[8,512,128]{2,1,0:T(8,128)(2,1)}) custom-call(s32[8,8]{1,0:T(8,128)} %bitcast.6, s32[6]{0:T(128)} %offsets_hbm.1, bf16[512,128]{1,0:T(8,128)(2,1)} %con_hbm.1, bf16[8,512,1024]{2,1,0:T(8,128)(2,1)} %bitcast.4, bf16[8,512,1024]{2,1,0:T(8,128)(2,1)} %bitcast.5, bf16[1024,256]{1,0:T(8,128)(2,1)} %proj_hbm.1, ...), custom_call_target="tpu_custom_call" | custom-call | tf_op jit(solution)/shard_map/pallas_call | solution.py:362
  33.4 6.0 %shard_map.96 = (bf16[8,512,1024]{2,1,0:T(8,128)(2,1)}, f32[512,128]{1,0:T(8,128)}) custom-call(bf16[8,512,256]{2,1,0:T(8,128)(2,1)} %get-tuple-element.6.loc_hbm, bf16[256,1024]{1,0:T(8,128)(2,1)} %expand_hbm.3, bf16[8,512,128]{2,1,0:T(8,128)(2,1)} %get-tuple-element.7.part_hbm), custom_call_target="tpu_custom_call" | custom-call | tf_op jit(solution)/shard_map/pallas_call | solution.py:405

commit v6 on v5

--- a/solution.py
+++ b/solution.py
@@ -25,6 +25,7 @@
 LANES = 128
 NZ = 4
 PEERS = [(1, 2), (1, 1), (1, 3), (0, 2), (1, 0), (0, 1), (0, 3)]
+HP = 1
 ET = 2
 
 
@@ -38,10 +39,10 @@
 
 def scatter_gradient_kernel(
     signs_hbm, offsets_hbm, con_hbm, inc_hbm, adj_hbm, proj_hbm, mats_hbm, expand_hbm,
-    loc_hbm, part_hbm,
+    loc_hbm, part_hbm, ready_hbm,
     signs, offsets, proj, mats, expand,
     con_v, inc_v, adj_v, coef_v, low_v, high_v, loc_v, first_v, term_v, enc_points, enc_coeffs,
-    small_sem, in_sem, adj_sem, con_sem, loc_sem, own_sem,
+    small_sem, in_sem, adj_sem, con_sem, loc_sem, own_sem, ready_sem,
     ag_send, ag_recv, rs_send, rs_recv, halo_send, halo_recv,
 ):
     g = lax.axis_index("group")
@@ -109,6 +110,10 @@
     def loc_copy(t):
         r = rows_of(t)
         return pltpu.make_async_copy(loc_v.at[:, r], loc_hbm.at[:, r], loc_sem)
+
+    def ready_copy(t):
+        to = pl.ds(pl.multiple_of((t - ET) * TB, TB), TB)
+        return pltpu.make_async_copy(inc_v.at[:, rows_of(t)], ready_hbm.at[:, to], ready_sem)
 
     def halo_up():
         return pltpu.make_async_remote_copy(
@@ -237,11 +242,17 @@
             for c in range(NC):
                 cols = pl.ds(c * CW, CW)
                 field = mm(local, expand[:, cols])
+                inc_v[:, boxes, cols] = field.astype(BF).reshape(S, HB, CW)
                 term = (weighted(boxes, cols, field) + first_v[boxes, cols]).astype(BF)
                 for q in range(CW // GW):
                     term_v[c * (CW // GW) + q, boxes, :] = term[:, q * GW : (q + 1) * GW]
         loc_copy(t).start()
         own_copy(t).start()
+
+        @pl.when((t >= ET) & (t < ET * (1 + HP)))
+        def _():
+            ready_copy(t).start()
+
         for k in range(1, NG):
             rs_copy(t, k).start()
 
@@ -290,6 +301,7 @@
     lax.fori_loop(0, NT + 2, step, 0)
 
     wait_bytes(loc_v, loc_sem)
+    wait_bytes(ready_hbm, ready_sem)
     wait_bytes(term_v.at[0], own_sem)
     wait_bytes(con_v.at[pl.ds(0, NG - 1)], ag_send)
     wait_bytes(term_v.at[pl.ds(0, NG - 1)], rs_send)
@@ -305,8 +317,9 @@
 
 
 def output_kernel(
-    loc_hbm, expand_hbm, part_hbm, scat_hbm, grad_hbm,
-    loc_v, expand, part_v, scat_v, grad_v, loc_sem, expand_sem, part_sem, scat_sem, grad_sem,
+    loc_hbm, expand_hbm, part_hbm, ready_hbm, scat_hbm, grad_hbm,
+    loc_v, expand, part_v, scat_v, grad_v,
+    loc_sem, expand_sem, part_sem, ready_sem, scat_sem, grad_sem,
 ):
     def rows_of(t):
         return pl.ds(pl.multiple_of(t * TB, TB), TB)
@@ -318,19 +331,26 @@
     def scat_copy(t, e):
         r = rows_of(t)
         return pltpu.make_async_copy(scat_v.at[e, r], scat_hbm.at[e, r], scat_sem)
+
+    def ready_copy(t):
+        src = ready_hbm.at[:, (t - ET) * TB : (t - ET + 1) * TB]
+        return pltpu.make_async_copy(src, scat_v.at[:, rows_of(t)], ready_sem.at[t - ET])
 
     expand_copy = pltpu.make_async_copy(expand_hbm, expand, expand_sem)
     part_copy = pltpu.make_async_copy(part_hbm, part_v, part_sem)
     grad_copy = pltpu.make_async_copy(grad_v, grad_hbm, grad_sem)
     loc_copy(0).start()
     expand_copy.start()
-    for t in range(1, NT):
+    loc_copy(1).start()
+    for t in range(ET, ET * (1 + HP)):
+        ready_copy(t).start()
+    for t in range(ET * (1 + HP), NT):
         loc_copy(t).start()
     part_copy.start()
     expand_copy.wait()
 
     def step(i, carry):
-        tiles = [ET * i + t for t in range(ET)]
+        tiles = [ET * jnp.where(i == 0, 0, i + HP) + t for t in range(ET)]
         for t in tiles:
             loc_copy(t).wait()
         for t in tiles:
@@ -343,7 +363,14 @@
             for e in range(S):
                 scat_copy(t, e).start()
 
-        @pl.when(i == NT // ET - 2)
+        @pl.when(i == 0)
+        def _():
+            for t in range(ET, ET * (1 + HP)):
+                ready_copy(t).wait()
+                for e in range(S):
+                    scat_copy(t, e).start()
+
+        @pl.when(i == NT // ET - HP - 2)
         def _():
             part_copy.wait()
             grad_v[...] = jnp.sum(part_v[...].astype(F32), axis=0)
@@ -351,7 +378,7 @@
 
         return carry
 
-    lax.fori_loop(0, NT // ET, step, 0)
+    lax.fori_loop(0, NT // ET - HP, step, 0)
     wait_bytes(scat_v, scat_sem)
     grad_copy.wait()
 
@@ -359,14 +386,15 @@
 def on_device(contrast, incident, signs, adjoint, proj, mats, offsets, expand):
     any_spec = pl.BlockSpec(memory_space=pl.ANY)
     dma = pltpu.SemaphoreType.DMA
-    local, parts = pl.pallas_call(
+    local, parts, ready = pl.pallas_call(
         scatter_gradient_kernel,
         out_shape=(
             jax.ShapeDtypeStruct((S, NB, K), BF),
             jax.ShapeDtypeStruct((NG, NB, GW), BF),
+            jax.ShapeDtypeStruct((S, HP * ET * TB, PTS), BF),
         ),
         in_specs=[any_spec] * 8,
-        out_specs=(any_spec, any_spec),
+        out_specs=(any_spec,) * 3,
         scratch_shapes=[
             pltpu.SMEM((S, S), jnp.int32),
             pltpu.SMEM(offsets.shape, jnp.int32),
@@ -391,6 +419,7 @@
             dma,
             dma,
             dma,
+            dma,
             dma((NT,)),
             dma,
             dma,
@@ -408,7 +437,7 @@
             jax.ShapeDtypeStruct((S, NB, PTS), BF),
             jax.ShapeDtypeStruct((NB, GW), F32),
         ),
-        in_specs=[any_spec] * 3,
+        in_specs=[any_spec] * 4,
         out_specs=(any_spec, any_spec),
         scratch_shapes=[
             pltpu.VMEM((S, NB, K), BF),
@@ -419,11 +448,12 @@
             dma((NT,)),
             dma,
             dma,
+            dma((HP * ET,)),
             dma,
             dma,
         ],
         compiler_params=pltpu.CompilerParams(vmem_limit_bytes=60 << 20),
-    )(local, expand, parts)
+    )(local, expand, parts, ready)
     return scattered[None], gradient
 
 

time: 39.5 us -> 39.4 us (level)
  no operation moved by 1% of the time
where the time goes in v6:
time: 39.4 us; the launch traced here: 39.3 us
  Pallas kernels  38.7 us (98%)
  between operations  0.64 us (2%)
    pallas_call x1, Pallas kernels, on_device(): pl.pallas_call(scatter_gradient_kernel, out_shape=(jax.ShapeDtypeStruct((...  32.8 us
    pallas_call x1, Pallas kernels, on_device(): pl.pallas_call(output_kernel, out_shape=(jax.ShapeDtypeStruct((S, NB, PTS...  5.91 us

profile of v6, /device:TPU:0, one launch (start us, length us, event | category | flops | bytes accessed | tf_op | source)
XLA Modules:
  0.0 39.3 jit_solution(3438305780977044798)
XLA Ops:
  0.6 32.8 %shard_map.95 = (bf16[8,512,256]{2,1,0:T(8,128)(2,1)}, bf16[8,512,128]{2,1,0:T(8,128)(2,1)}, bf16[8,128,1024]{2,1,0:T(8,128)(2,1)}) custom-call(s32[8,8]{1,0:T(8,128)} %bitcast.6, s32[6]{0:T(128)} %offsets_hbm.1, bf16[512,128]{1,0:T(8,128)(2,1)} %con_hbm.1, bf16[8,512,1024]{2,1,0:T(8,128)(2,1)} %bitcast.4, bf16[8,512,1024]{2,1,0:T(8,128)(2,1)} %bitcast.5, ...), custom_call_target="tpu_custom_call" | custom-call | tf_op jit(solution)/shard_map/pallas_call | solution.py:389
  33.4 5.9 %shard_map.96 = (bf16[8,512,1024]{2,1,0:T(8,128)(2,1)}, f32[512,128]{1,0:T(8,128)}) custom-call(bf16[8,512,256]{2,1,0:T(8,128)(2,1)} %get-tuple-element.7.loc_hbm, bf16[256,1024]{1,0:T(8,128)(2,1)} %expand_hbm.3, bf16[8,512,128]{2,1,0:T(8,128)(2,1)} %get-tuple-element.8.part_hbm, bf16[8,128,1024]{2,1,0:T(8,128)(2,1)} %get-tuple-element.9.ready_hbm), custom_call_target="tpu_custom_call" | custom-call | tf_op jit(solution)/shard_map/pallas_call | solution.py:434
